TPU v7x, 128 devices: a whole 4x4x4 slice. The times are simulated.
128 devices in a mesh: row: 8 (over y, core), col: 16 (over z, x).
Axes of the slice: x: 4, y: 4, z: 4, core: 2. Of those that a mesh axis runs over, the one named last changes fastest.
Arguments:
- rhs: float32 [64, 65536], P(None, ('row', 'col')), may hold values from -6 to 6
- self_term: float32 [65536], P(('row', 'col')), may hold values from 4 to 6
- near_tiles: bfloat16 [16384, 256, 256], P(('row', 'col')), may hold values from -0.0241 to 0.0241
- near_rows: int32 [16384], P(('row', 'col')), may hold values from 0 to 31
- near_cols: int32 [16384], P(('row', 'col')), may hold values from 0 to 15
- near_counts: int32 [128], replicated, may hold values from 1 to 128, as said below
- far_left: bfloat16 [8192, 256, 32], P(('row', 'col')), may hold values from -0.125 to 0.125
- far_right: bfloat16 [8192, 256, 32], P(('row', 'col')), may hold values from -0.125 to 0.125
- far_rows: int32 [8192], P(('row', 'col')), may hold values from 0 to 31
- far_cols: int32 [8192], P(('row', 'col')), may hold values from 0 to 15
- nys_factor: float32 [512, 65536], P(None, ('row', 'col')), may hold values from -0.0234375 to 0.0234375
- nys_weight: float32 [512], replicated, may hold values from 1 to 16
Outputs:
- solution: float32 [64, 65536], P(None, ('row', 'col'))
- residual: float32 [64, 65536], P(None, ('row', 'col'))
Inputs may be any that keep to these rules, and one draw needn't show every extreme that they name: Owner o uses its first near_counts[o] slots; some owner uses all 128.
All inputs are finite; a program needn't handle non-finite values.
Results may differ from a plain program's by a relative error of at most 0.0003.
Values may be sent and summed in bfloat16 or wider, within the bound.
A program may use at most 128 MiB of HBM per device.

v0:
```python
import jax
import jax.numpy as jnp
from jax import lax
from jax.sharding import PartitionSpec as P

ITERS = 2


def chol_solve(matrix, target):
    return jax.scipy.linalg.cho_solve((jnp.linalg.cholesky(matrix), True), target)


def local(
    rhs,
    self_term,
    near_tiles,
    near_rows,
    near_cols,
    near_counts,
    far_left,
    far_right,
    far_rows,
    far_cols,
    nys_factor,
    nys_weight,
):
    highest = lax.Precision.HIGHEST
    width = near_tiles.shape[1]
    rhs_count = rhs.shape[0]
    group = 8
    n_col = lax.axis_size("col")
    grid_row = lax.axis_index("row")
    grid_col = lax.axis_index("col")
    count = near_counts[grid_row * n_col + grid_col]

    def precondition(resid):
        local_proj = jnp.dot(resid, nys_factor.T, precision=highest)
        proj = lax.psum(local_proj, ("row", "col"))
        precond = resid + jnp.dot(proj * nys_weight, nys_factor, precision=highest)
        rho_value = lax.psum(jnp.dot(resid, precond.T, precision=highest), ("row", "col"))
        return (precond, rho_value)

    solution = jnp.zeros_like(rhs)
    residual = rhs
    precond, rho = precondition(residual)
    direc = precond
    for step in range(ITERS):
        packed = direc.astype(jnp.bfloat16)
        col_side = lax.all_gather(packed, "row", axis=1, tiled=True)
        row_side = lax.all_gather(packed, "col", axis=1, tiled=True)
        col_blocks = col_side.reshape(rhs_count, -1, width).transpose(1, 0, 2)
        row_blocks = row_side.reshape(rhs_count, -1, width).transpose(1, 0, 2)
        ids = jnp.arange(group, dtype=jnp.int32)

        def forward_step(index, acc):
            start = index * group
            tiles = lax.dynamic_slice_in_dim(near_tiles, start, group, 0)
            rows = lax.dynamic_slice_in_dim(near_rows, start, group, 0)
            cols = lax.dynamic_slice_in_dim(near_cols, start, group, 0)
            prod = jnp.einsum(
                "gmk,gnk->gmn", col_blocks[cols], tiles, preferred_element_type=jnp.float32
            )
            valid = (start + ids < count)[:, None, None]
            return acc.at[rows].add(jnp.where(valid, prod, 0.0))

        def transposed_step(index, acc):
            start = index * group
            tiles = lax.dynamic_slice_in_dim(near_tiles, start, group, 0)
            rows = lax.dynamic_slice_in_dim(near_rows, start, group, 0)
            cols = lax.dynamic_slice_in_dim(near_cols, start, group, 0)
            prod = jnp.einsum(
                "gmn,gnk->gmk", row_blocks[rows], tiles, preferred_element_type=jnp.float32
            )
            valid = (start + ids < count)[:, None, None]
            return acc.at[cols].add(jnp.where(valid, prod, 0.0))

        forward = jnp.zeros((row_blocks.shape[0], rhs_count, width), jnp.float32)
        forward = lax.fori_loop(0, (count + group - 1) // group, forward_step, forward)
        transposed = jnp.zeros((col_blocks.shape[0], rhs_count, width), jnp.float32)
        transposed = lax.fori_loop(0, (count + group - 1) // group, transposed_step, transposed)
        half_f = jnp.einsum(
            "fmk,fkr->fmr", col_blocks[far_cols], far_right, preferred_element_type=jnp.float32
        ).astype(jnp.bfloat16)
        half_t = jnp.einsum(
            "fmn,fnr->fmr", row_blocks[far_rows], far_left, preferred_element_type=jnp.float32
        ).astype(jnp.bfloat16)
        forward = forward.at[far_rows].add(
            jnp.einsum("fmr,fnr->fmn", half_f, far_left, preferred_element_type=jnp.float32)
        )
        transposed = transposed.at[far_cols].add(
            jnp.einsum("fmr,fkr->fmk", half_t, far_right, preferred_element_type=jnp.float32)
        )
        row_terms = forward.transpose(1, 0, 2).reshape(rhs_count, -1)
        col_terms = transposed.transpose(1, 0, 2).reshape(rhs_count, -1)
        row_result = lax.psum_scatter(row_terms, "col", scatter_dimension=1, tiled=True)
        col_result = lax.psum_scatter(col_terms, "row", scatter_dimension=1, tiled=True)
        image = self_term * direc + row_result + col_result
        gram = lax.psum(jnp.dot(direc, image.T, precision=highest), ("row", "col"))
        alpha = chol_solve(gram, rho)
        solution = solution + jnp.dot(alpha.T, direc, precision=highest)
        residual = residual - jnp.dot(alpha.T, image, precision=highest)
        if step + 1 < ITERS:
            precond, rho_next = precondition(residual)
            beta = chol_solve(rho, rho_next)
            direc = precond + jnp.dot(beta.T, direc, precision=highest)
            rho = rho_next
    return (solution, residual)


def solution(mesh):
    in_specs = (
        P(None, ("row", "col")),
        P(("row", "col")),
        P(("row", "col"), None, None),
        P(("row", "col")),
        P(("row", "col")),
        P(),
        P(("row", "col"), None, None),
        P(("row", "col"), None, None),
        P(("row", "col")),
        P(("row", "col")),
        P(None, ("row", "col")),
        P(),
    )
    out_specs = (P(None, ("row", "col")), P(None, ("row", "col")))
    return jax.shard_map(local, mesh=mesh, in_specs=in_specs, out_specs=out_specs, check_vma=False)
```

profile of v0, /device:TPU:0, one launch (start us, length us, event | category | flops | bytes accessed | tf_op | source)
XLA Modules:
  0.0 1210.9 jit_solution(12687977982972929271)
XLA Ops:
  7.3 3.2 fusion.50
  10.5 147.4 %all-reduce.4.cloned.1.call-done = f32[64,512]{1,0:T(8,128)} async-done(((f32[64,512]{1,0:T(8,128)}), f32[64,512]{1,0:T(8,128)}) %all-reduce.4.cloned.1.call-update) | async-done | bytes 131088 | tf_op jit(solution)/shard_map/psum | solution.py:38
  157.9 2.4 fusion.48
  162.3 13.3 %all_gather.12 = bf16[64,4096]{1,0:T(8,128)(2,1)S(1)} all-gather(bf16[64,512]{1,0:T(8,128)(2,1)} %get-tuple-element.350), channel_id=1, replica_groups=mesh['row'=8,'col'=16] {'row'}, dimensions={1}, use_global_device_ids=true | all-gather | bytes 589824 | tf_op jit(solution)/shard_map/all_gather | solution.py:49
  177.8 4.7 fusion.20
  182.5 18.7 %all-gather.3.cloned.1.call-done = bf16[64,8192]{1,0:T(8,128)(2,1)} async-done(((bf16[64,512]{1,0:T(8,128)(2,1)}), bf16[64,8192]{1,0:T(8,128)(2,1)}) %all-gather.3.cloned.1.call-update) | async-done | bytes 1048592 | tf_op jit(solution)/shard_map/all_gather | solution.py:50
  201.2 2.3 copy.42
  203.7 20.7 %while.45 = (s32[]{:T(128)}, f32[16,64,256]{2,1,0:T(8,128)S(1)}, s32[]{:T(128)}, s32[128]{0:T(128)S(1)}, s32[]{:T(128)}, /*index=5*/s32[128]{0:T(128)S(1)}, bf16...) while((s32[]{:T(128)}, f32[16,64,256]{2,1,0:T(8,128)S(1)}, ...), condition=%wide.region_8.9_spmd.clone, body=%wide.region_6.8_spmd.clone.sunk | while | flops 67372104 | bytes 3936683 | solution.py:80
  224.4 3.4 gather_fusion.5
  227.8 4.8 fusion.21
  232.6 8.8 scatter_fusion.5
  242.8 27.7 %while.44 = (s32[]{:T(128)}, f32[32,64,256]{2,1,0:T(8,128)S(1)}, s32[]{:T(128)}, s32[128]{0:T(128)S(1)}, s32[]{:T(128)}, /*index=5*/s32[128]{0:T(128)S(1)}, bf16...) while((s32[]{:T(128)}, f32[32,64,256]{2,1,0:T(8,128)S(1)}, ...), condition=%wide.region_3.4_spmd.clone, body=%wide.region_1.3_spmd.clone.sunk | while | flops 67372104 | bytes 3936683 | solution.py:78
  245.2 2.5 convolution_select_fusion.8
  252.1 2.5 convolution_select_fusion.8
  254.6 2.0 scatter_fusion
  259.0 2.5 convolution_select_fusion.8
  261.5 2.0 scatter_fusion
  265.9 2.5 convolution_select_fusion.8
  268.4 2.0 scatter_fusion
  270.4 8.9 scatter_fusion.4
  282.1 51.7 %reduce-scatter.7.cloned.1.call-done = f32[64,512]{1,0:T(8,128)} async-done(((f32[64,4096]{1,0:T(8,128)}), f32[64,512]{1,0:T(8,128)}) %reduce-scatter.7.cloned.1.call-update) | async-done | bytes 131088 | tf_op jit(solution)/shard_map/reduce_scatter | solution.py:96
  333.8 164.6 %reduce-scatter.5.cloned.1.call-done = f32[64,512]{1,0:T(8,128)} async-done(((f32[64,8192]{1,0:T(8,128)}), f32[64,512]{1,0:T(8,128)}) %reduce-scatter.5.cloned.1.call-update) | async-done | bytes 131088 | tf_op jit(solution)/shard_map/reduce_scatter | solution.py:95
  499.6 65.2 %all-reduce = (f32[64,64]{0,1:T(8,128)S(1)}, f32[64,64]{0,1:T(8,128)S(1)}) all-reduce(f32[64,64]{0,1:T(8,128)S(1)} %convolution_bitcast_fusion, f32[64,64]{0,1:T(8,128)S(1)} %fusion.28), channel_id=1, replica_groups=mesh['row'=8,'col'=16] {'row','col'}, use_global_device_ids=true, to_apply=%region_14.16 | all-reduce | flops 8192 | bytes 65536 | tf_op jit(solution)/shard_map/psum | solution.py:40
  565.0 5.8 cholesky.59
  572.2 4.9 custom-call.9
  580.7 5.8 cholesky.70
  587.9 4.9 custom-call.10
  592.8 126.3 %all-reduce.6.cloned.1.call-done = f32[64,512]{1,0:T(8,128)} async-done(((f32[64,512]{1,0:T(8,128)}), f32[64,512]{1,0:T(8,128)}) %all-reduce.6.cloned.1.call-update) | async-done | bytes 131088 | tf_op jit(solution)/shard_map/psum | solution.py:38
  721.0 63.6 %psum.46 = f32[64,64]{1,0:T(8,128)S(1)} all-reduce(f32[64,64]{1,0:T(8,128)S(1)} %fusion.53), channel_id=1, replica_groups=mesh['row'=8,'col'=16] {'row','col'}, use_global_device_ids=true, to_apply=%region_16.19 | all-reduce | flops 4096 | bytes 32768 | tf_op jit(solution)/shard_map/psum | solution.py:40
  786.1 13.3 %all_gather.14 = bf16[64,4096]{1,0:T(8,128)(2,1)S(1)} all-gather(bf16[64,512]{1,0:T(8,128)(2,1)} %get-tuple-element.352), channel_id=1, replica_groups=mesh['row'=8,'col'=16] {'row'}, dimensions={1}, use_global_device_ids=true | all-gather | bytes 589824 | tf_op jit(solution)/shard_map/all_gather | solution.py:49
  799.5 2.3 gather_fusion.6
  801.7 4.7 fusion.22
  806.5 19.5 %all-gather.5.cloned.1.call-done = bf16[64,8192]{1,0:T(8,128)(2,1)} async-done(((bf16[64,512]{1,0:T(8,128)(2,1)}), bf16[64,8192]{1,0:T(8,128)(2,1)}) %all-gather.5.cloned.1.call-update) | async-done | bytes 1048592 | tf_op jit(solution)/shard_map/all_gather | solution.py:50
  828.3 2.2 gather_fusion.7
  830.6 20.9 %while.47 = (s32[]{:T(128)}, f32[16,64,256]{2,1,0:T(8,128)S(1)}, s32[]{:T(128)}, s32[128]{0:T(128)S(1)}, s32[]{:T(128)}, /*index=5*/s32[128]{0:T(128)S(1)}, bf16...) while((s32[]{:T(128)}, f32[16,64,256]{2,1,0:T(8,128)S(1)}, ...), condition=%wide.region_24.27_spmd.clone, body=%wide.region_22.26_spmd.clone.sunk | while | flops 67372104 | bytes 3936683 | solution.py:80
  851.6 5.0 fusion.23
  856.6 8.8 scatter_fusion.7
  866.8 27.7 %while.46 = (s32[]{:T(128)}, f32[32,64,256]{2,1,0:T(8,128)S(1)}, s32[]{:T(128)}, s32[128]{0:T(128)S(1)}, s32[]{:T(128)}, /*index=5*/s32[128]{0:T(128)S(1)}, bf16...) while((s32[]{:T(128)}, f32[32,64,256]{2,1,0:T(8,128)S(1)}, ...), condition=%wide.region_19.22_spmd.clone, body=%wide.region_17.21_spmd.clone.sunk | while | flops 67372104 | bytes 3936683 | solution.py:78
  869.2 2.5 convolution_select_fusion.10
  876.1 2.5 convolution_select_fusion.10
  883.0 2.5 convolution_select_fusion.10
  890.0 2.5 convolution_select_fusion.10
  894.5 8.9 scatter_fusion.6
  906.0 51.8 %reduce-scatter.11.cloned.1.call-done = f32[64,512]{1,0:T(8,128)} async-done(((f32[64,4096]{1,0:T(8,128)}), f32[64,512]{1,0:T(8,128)}) %reduce-scatter.11.cloned.1.call-update) | async-done | bytes 131088 | tf_op jit(solution)/shard_map/reduce_scatter | solution.py:96
  957.8 164.6 %reduce-scatter.9.cloned.1.call-done = f32[64,512]{1,0:T(8,128)} async-done(((f32[64,8192]{1,0:T(8,128)}), f32[64,512]{1,0:T(8,128)}) %reduce-scatter.9.cloned.1.call-update) | async-done | bytes 131088 | tf_op jit(solution)/shard_map/reduce_scatter | solution.py:95
  1123.7 64.8 %psum.47 = f32[64,64]{0,1:T(8,128)S(1)} all-reduce(f32[64,64]{0,1:T(8,128)S(1)} %fusion.29), channel_id=1, replica_groups=mesh['row'=8,'col'=16] {'row','col'}, use_global_device_ids=true, to_apply=%region_27.30 | all-reduce | flops 4096 | bytes 32768 | tf_op jit(solution)/shard_map/psum | solution.py:98
  1188.6 5.8 cholesky.81
  1195.8 4.9 custom-call.11
  (209 shorter events, 101.0 us)
Async XLA Ops:
  7.2 170.6 %copy-start = (bf16[64,256,32]{1,2,0:T(8,128)(2,1)S(1)}, bf16[64,256,32]{1,2,0:T(8,128)(2,1)}, u32[]{:S(2)}) copy-start(bf16[64,256,32]{1,2,0:T(8,128)(2,1)} %param.30) | copy-start | bytes 3145732
  7.2 150.7 %copy-start.4 = (f32[512,512]{1,0:T(8,128)S(1)}, f32[512,512]{1,0:T(8,128)}, u32[]{:S(2)}) copy-start(f32[512,512]{1,0:T(8,128)} %param.33) | copy-start | bytes 3145732
  7.2 153.2 %copy-start.27 = (s32[128]{0:T(128)S(1)}, s32[128]{0:T(128)}, u32[]{:S(2)}) copy-start(s32[128]{0:T(128)} %param.28) | copy-start | bytes 1540
  7.2 154.5 %copy-start.28 = (s32[64]{0:T(128)S(1)}, s32[64]{0:T(128)}, u32[]{:S(2)}) copy-start(s32[64]{0:T(128)} %param.31) | copy-start | bytes 772
  7.2 155.1 %copy-start.29 = (s32[64]{0:T(128)S(1)}, s32[64]{0:T(128)}, u32[]{:S(2)}) copy-start(s32[64]{0:T(128)} %param.32) | copy-start | bytes 772
  7.2 150.7 %all-reduce.4.cloned.1.call-start = ((), (), s32[]{:S(2)}) async-start(), calls=%async_computation.4 | async-start | bytes 262144 | tf_op jit(solution)/shard_map/psum | solution.py:38
  10.5 190.8 %all-gather.3.cloned.1.call-start = ((), (), s32[]{:S(2)}) async-start(), calls=%async_computation.6 | async-start | bytes 1114112 | tf_op jit(solution)/shard_map/all_gather | solution.py:50
  160.3 173.4 %reduce-scatter.7.cloned.1.call-start = ((), (), s32[]{:S(2)}) async-start(), calls=%async_computation.7 | async-start | bytes 1179648 | tf_op jit(solution)/shard_map/reduce_scatter | solution.py:96
  161.8 0.5 copy-start.24
  162.3 62.1 %copy-start.22 = (s32[1024]{0:T(1024)}, s32[1024]{0:T(1024)S(1)}, u32[]{:S(2)}) copy-start(s32[1024]{0:T(1024)S(1)} %pad_clamp_fusion.4) | copy-start | bytes 12292
  162.3 70.2 %copy-start.25 = (s32[64]{0:T(128)}, s32[64]{0:T(128)S(1)}, u32[]{:S(2)}) copy-start(s32[64]{0:T(128)S(1)} %compare_select_fusion.8) | copy-start | bytes 772
  162.3 15.4 %copy-start.23 = (s32[1024]{0:T(1024)}, s32[1024]{0:T(1024)S(1)}, u32[]{:S(2)}) copy-start(s32[1024]{0:T(1024)S(1)} %pad_clamp_fusion.5) | copy-start | bytes 12292
  175.7 2.0 copy-start.2
  175.7 2.0 copy-start.6
  182.5 21.1 %copy-start.17 = (s32[128]{0:T(128)S(1)}, s32[128]{0:T(128)}, u32[]{:S(2)}) copy-start(s32[128]{0:T(128)} %param.27) | copy-start | bytes 1540
  182.5 21.2 %copy-start.18 = (s32[128]{0:T(128)S(1)}, s32[128]{0:T(128)}, u32[]{:S(2)}) copy-start(s32[128]{0:T(128)} %param.26) | copy-start | bytes 1540
  224.4 3.4 copy-start.7
  242.5 255.9 %reduce-scatter.5.cloned.1.call-start = ((), (), s32[]{:S(2)}) async-start(), calls=%async_computation.5 | async-start | bytes 2228224 | tf_op jit(solution)/shard_map/reduce_scatter | solution.py:95
  280.9 0.9 copy-start.12
  280.9 217.5 %copy-start.19 = (f32[512]{0:T(512)S(1)}, f32[512]{0:T(512)}, u32[]{:S(2)}) copy-start(f32[512]{0:T(512)} %param.24) | copy-start | bytes 6148
  280.9 297.9 %copy-start.5 = (f32[512,512]{1,0:T(8,128)S(1)}, f32[512,512]{1,0:T(8,128)}, u32[]{:S(2)}) copy-start(f32[512,512]{1,0:T(8,128)} %param.33) | copy-start | bytes 3145732
  281.0 438.1 %copy-start.21 = (f32[512]{0:T(512)S(1)}, f32[512]{0:T(512)}, u32[]{:S(2)}) copy-start(f32[512]{0:T(512)} %param.34) | copy-start | bytes 6148
  281.0 438.1 %all-reduce.6.cloned.1.call-start = ((), (), s32[]{:S(2)}) async-start(), calls=%async_computation.8 | async-start | bytes 262144 | tf_op jit(solution)/shard_map/psum | solution.py:38
  577.5 207.4 %copy-start.15 = (f32[64,64]{1,0:T(8,128)}, f32[64,64]{1,0:T(8,128)S(1)}, u32[]{:S(2)}) copy-start(f32[64,64]{1,0:T(8,128)S(1)} %fusion.43) | copy-start | bytes 49156
  578.9 220.5 %copy-start.9 = (f32[64,512]{1,0:T(8,128)}, f32[64,512]{1,0:T(8,128)S(1)}, u32[]{:S(2)}) copy-start(f32[64,512]{1,0:T(8,128)S(1)} %convolution_subtract_fusion.1) | copy-start | bytes 393220
  580.7 245.3 %all-gather.5.cloned.1.call-start = ((), (), s32[]{:S(2)}) async-start(), calls=%async_computation.10 | async-start | bytes 1114112 | tf_op jit(solution)/shard_map/all_gather | solution.py:50
  784.6 14.8 %copy-start.13 = (f32[64,64]{1,0:T(8,128)}, f32[64,64]{1,0:T(8,128)S(1)}, u32[]{:S(2)}) copy-start(f32[64,64]{1,0:T(8,128)S(1)} %psum.46) | copy-start | bytes 49156
  786.0 171.8 %reduce-scatter.11.cloned.1.call-start = ((), (), s32[]{:S(2)}) async-start(), calls=%async_computation.11 | async-start | bytes 1179648 | tf_op jit(solution)/shard_map/reduce_scatter | solution.py:96
  799.4 2.3 copy-start.1
  799.4 2.3 copy-start.8
  827.4 1.0 copy-start.3
  851.5 5.1 copy-start.26
  866.5 255.9 %reduce-scatter.9.cloned.1.call-start = ((), (), s32[]{:S(2)}) async-start(), calls=%async_computation.9 | async-start | bytes 2228224 | tf_op jit(solution)/shard_map/reduce_scatter | solution.py:95
  905.0 0.8 copy-start.16
  905.0 217.5 %copy-start.11 = (f32[64,512]{1,0:T(8,128)S(1)}, f32[64,512]{1,0:T(8,128)}, u32[]{:S(2)}) copy-start(f32[64,512]{1,0:T(8,128)} %get-tuple-element.353) | copy-start | bytes 393220
  905.0 217.5 %copy-start.20 = (f32[512]{0:T(512)S(1)}, f32[512]{0:T(512)}, u32[]{:S(2)}) copy-start(f32[512]{0:T(512)} %param.24) | copy-start | bytes 6148
  905.0 295.7 %copy-start.14 = (f32[64,64]{1,0:T(8,128)S(1)}, f32[64,64]{1,0:T(8,128)}, u32[]{:S(2)}) copy-start(f32[64,64]{1,0:T(8,128)} %copy-done.13) | copy-start | bytes 49156
  905.0 297.1 %copy-start.10 = (f32[64,512]{1,0:T(8,128)S(1)}, f32[64,512]{1,0:T(8,128)}, u32[]{:S(2)}) copy-start(f32[64,512]{1,0:T(8,128)} %copy-done.9) | copy-start | bytes 393220
Sparse Core Ops, SparseCore 0:
  13.3 144.5 all-reduce.3
  160.6 40.5 all-gather.2
  242.6 91.1 reduce-scatter.6
  336.9 161.4 reduce-scatter.4
  580.8 138.2 all-reduce.5
  786.1 39.8 all-gather.4
  866.6 91.1 reduce-scatter.10
  961.1 161.3 reduce-scatter.8
where the time goes:
time: 1220 us; the launch traced here: 1210 us
  waiting for transfers between devices  745 us (61%)
  blocking collectives  220 us (18%)
  other arithmetic  108 us (9%)
  matrix products  70.1 us (6%)
  local copies, waits for them, and re-layouts  50.7 us (4%)
  between operations  15.4 us (1%)
    reduce_scatter x2, waiting for transfers between devices, local(): lax.psum_scatter(row_terms, 'col', scatter_dimension=1, tiled=True)  329 us
    psum x2, waiting for transfers between devices, precondition(): proj = lax.psum(local_proj, ('row', 'col'))  274 us
    psum x2, blocking collectives, precondition(): lax.psum(jnp.dot(resid, precond.T, precision=highest), ('row', 'col'))  129 us
    reduce_scatter x2, waiting for transfers between devices, local(): lax.psum_scatter(col_terms, 'row', scatter_dimension=1, tiled=True)  103 us
    psum x1, blocking collectives, local(): gram = lax.psum(jnp.dot(direc, image.T, precision=highest), ('row', 'col'))  64.8 us
    all_gather x2, waiting for transfers between devices, local(): row_side = lax.all_gather(packed, 'col', axis=1, tiled=True)  38.3 us
    all_gather x2, blocking collectives, local(): col_side = lax.all_gather(packed, 'row', axis=1, tiled=True)  26.6 us
  transfers between devices with their start and end apart: 8, of which 8 were waited for; matrix products, arithmetic and copies ran while one was open for 9% of the time, Pallas kernels for 0%

commit v1 on v0

v1 whole, which is shorter than its diff:
```python
import functools

import jax
import jax.numpy as jnp
from jax import lax
from jax.experimental import pallas as pl
from jax.experimental.pallas import tpu as pltpu
from jax.sharding import PartitionSpec as P

MESH = pl.DeviceIdType.MESH
HI = lax.Precision.HIGHEST
F32 = jnp.float32
BF16 = jnp.bfloat16
VMEM = pl.BlockSpec(memory_space=pltpu.VMEM)
SMEM = pl.BlockSpec(memory_space=pltpu.SMEM)
ANY = pl.BlockSpec(memory_space=pl.ANY)
NT = (((1,), (1,)), ((), ()))
NN = (((1,), (0,)), ((), ()))
TN = (((0,), (0,)), ((), ()))
M = 64
B = 256
D = 512
WIDE = 640
GROUP = 8


def dot(a, b, dims=NN, precision=None):
    return lax.dot_general(a, b, dims, precision=precision, preferred_element_type=F32)


class Net:
    def __init__(self, send, recv):
        self.send, self.recv, self.used = send, recv, 0
        self.i, self.j = lax.axis_index("row"), lax.axis_index("col")
        self.y, self.core = self.i // 2, self.i % 2
        self.z, self.x = self.j // 4, self.j % 4

    def partner(self):
        return (self.y * 2 + 1 - self.core, self.j)

    def at(self, axis, step):
        if axis == "y":
            return ((self.y + step) % 4 * 2 + self.core, self.j)
        if axis == "z":
            return (self.i, (self.z + step) % 4 * 4 + self.x)
        return (self.i, self.z * 4 + (self.x + step) % 4)

    def barrier(self):
        sem = pltpu.get_barrier_semaphore()
        peers = [self.partner()] + [self.at(a, s) for a in "xyz" for s in (1, 2, 3)]
        for peer in peers:
            pl.semaphore_signal(sem, inc=1, device_id=peer, device_id_type=MESH)
        pl.semaphore_wait(sem, len(peers))

    def copy(self, src, dst, device):
        k = self.used
        self.used += 1
        c = pltpu.make_async_remote_copy(
            src_ref=src,
            dst_ref=dst,
            send_sem=self.send.at[k],
            recv_sem=self.recv.at[k],
            device_id=device,
            device_id_type=MESH,
        )
        c.start()
        return c


def rows(start, size):
    return pl.ds(pl.multiple_of(start, 8), size)


def exchange(net, axis, src, slots):
    return [net.copy(src, slots.at[d - 1], net.at(axis, d)) for d in (1, 2, 3)]


def wait_all(copies):
    for c in copies:
        c.wait()


def all_reduce_wide(net, part, total, core_in, y_in, x_own, x_in, z_own, z_in):
    other, own = (1 - net.core) * 32, net.core * 32
    net.copy(part.at[rows(other, 32)], core_in, net.partner()).wait()
    core_in[...] += part[rows(own, 32), :]
    copies = [
        net.copy(core_in.at[rows((net.y + d) % 4 * 8, 8)], y_in.at[d - 1], net.at("y", d))
        for d in (1, 2, 3)
    ]
    wait_all(copies)
    x_own[...] = core_in[rows(net.y * 8, 8), :] + y_in[0] + y_in[1] + y_in[2]
    wait_all(exchange(net, "x", x_own, x_in))
    z_own[...] = x_own[...] + x_in[0] + x_in[1] + x_in[2]
    wait_all(exchange(net, "z", z_own, z_in))
    mine = rows(own + net.y * 8, 8)
    total[mine, :] = z_own[...] + z_in[0] + z_in[1] + z_in[2]
    copies = [net.copy(total.at[mine], total.at[mine], net.at("y", d)) for d in (1, 2, 3)]
    wait_all(copies)
    half = rows(own, 32)
    net.copy(total.at[half], total.at[half], net.partner()).wait()


def project(resid, factor, part):
    part[:, 0:D] = dot(resid, factor[...], NT, HI)
    part[:, D:] = jnp.concatenate([dot(resid, resid, NT, HI), jnp.zeros((M, M), F32)], 1)


def precondition(resid, factor, weight, total):
    proj = total[:, 0:D]
    weighted = proj * weight[...]
    precond = resid + dot(weighted, factor[...], NN, HI)
    rho = total[:, D : D + M] + dot(weighted, proj, NT, HI)
    return precond, rho


def gather(net, direc, rowb, colb):
    y, z, x, core = net.y, net.z, net.x, net.core
    for b in (0, 1):
        block = direc[:, b * B : (b + 1) * B].astype(BF16)
        rowb[z, x, b] = block
        colb[y, core, b] = block
    lo, hi = pl.ds(0, 32), pl.ds(32, 32)

    def blk(b, first, second):
        return (((z + second) % 4, (x + first) % 4) if b == 0 else ((z + first) % 4, (x + second) % 4)) + (b,)

    firsts, seconds = ("x", "z"), ("z", "x")
    done = []

    def send(ref, device):
        c = net.copy(ref, ref, device)
        done.append(c)
        return c

    one = {}
    for b in (0, 1):
        ref = rowb.at[blk(b, 0, 0)]
        one[b] = [send(ref, net.at(firsts[b], 1)), send(ref, net.at(firsts[b], -1))]
    ref = colb.at[y, core]
    col_one = [send(ref, net.at("y", 1)), send(ref, net.at("y", -1))]
    col_core = [send(ref, net.partner())]

    two, second = {}, {0: {}, 1: {}}

    def spread(b, first):
        ref = rowb.at[blk(b, first, 0)]
        second[b][first] = [send(ref, net.at(seconds[b], 1)), send(ref, net.at(seconds[b], -1))]

    for b in (0, 1):
        spread(b, 0)
    for b in (0, 1):
        one[b][0].wait_recv()
        before = rowb.at[blk(b, -1, 0)]
        two[b] = [send(before.at[lo], net.at(firsts[b], 1))]
        one[b][1].wait_recv()
        after = rowb.at[blk(b, 1, 0)]
        two[b].append(send(after.at[hi], net.at(firsts[b], -1)))
    col_one[0].wait_recv()
    col_two = [send(colb.at[(y + 3) % 4, core, 0], net.at("y", 1))]
    col_one[1].wait_recv()
    col_two.append(send(colb.at[(y + 1) % 4, core, 1], net.at("y", -1)))
    for b in (0, 1):
        spread(b, -1)
        spread(b, 1)
    for step in (-1, 1):
        col_core.append(send(colb.at[(y + step) % 4, core], net.partner()))
    last = []

    def relay(b, first):
        up, down = second[b][first]
        up.wait_recv()
        ref = rowb.at[blk(b, first, -1)]
        last.append(send(ref.at[lo], net.at(seconds[b], 1)))
        down.wait_recv()
        ref = rowb.at[blk(b, first, 1)]
        last.append(send(ref.at[hi], net.at(seconds[b], -1)))

    for b in (0, 1):
        relay(b, 0)
    for b in (0, 1):
        two[b][0].wait_recv()
        two[b][1].wait_recv()
        spread(b, 2)
    for c in col_two:
        c.wait_recv()
    col_core.append(send(colb.at[(y + 2) % 4, core], net.partner()))
    for first in (-1, 1, 2):
        for b in (0, 1):
            relay(b, first)
    for c in last + col_core:
        c.wait_recv()
    for c in done:
        c.wait_send()


class Ring:
    def __init__(self, net, axis, chunk, via, direct, final):
        self.net, self.axis, self.chunk = net, axis, chunk
        self.via, self.direct, self.final = via, direct, final
        self.done = []

    def send(self, src, dst, step):
        c = self.net.copy(src, dst, self.net.at(self.axis, step))
        self.done.append(c)
        return c

    def start(self):
        chunk = self.chunk
        self.one = [self.send(chunk(2, 0), self.via.at[0], 1), self.send(chunk(2, 1), self.via.at[1], -1)]
        self.straight = [
            self.send(chunk(1, 1), self.direct.at[1], 1),
            self.send(chunk(-1, 0), self.direct.at[0], -1),
        ]

    def forward(self):
        self.two = []
        for half, step in ((0, 1), (1, -1)):
            self.one[half].wait_recv()
            self.via[half] += self.chunk(step, half)[...]
            self.two.append(self.send(self.via.at[half], self.final.at[half], step))

    def result(self, half):
        self.two[half].wait_recv()
        self.straight[1 - half].wait_recv()
        return self.final[half] + self.direct[half]

    def close(self):
        for c in self.done:
            c.wait_send()


def solve(left, right, eye=None):
    table = jnp.concatenate([left, right], 1)
    row_ids = lax.broadcasted_iota(jnp.int32, (M, 2 * M), 0)
    for k in range(M):
        pivot = table[k : k + 1, :] * (1.0 / table[k : k + 1, k : k + 1])
        column = jnp.where(row_ids[:, 0:1] == k, 0.0, table[:, k : k + 1])
        table = jnp.where(row_ids == k, pivot, table - column * pivot)
    return table[:, M:]


def scatter_sums(net, fwd, trans, bufs, beside):
    via_a, dir_a, fin_a, mid, via_b, dir_b, fin_b, core_in, via_y, dir_y, fin_y = bufs
    y, z, x, core = net.y, net.z, net.x, net.core
    half = (pl.ds(0, 32), pl.ds(32, 32))

    def first_chunk(b):
        if b == 0:
            return lambda step, h: fwd.at[:, (x + step) % 4, 0, half[h]]
        return lambda step, h: fwd.at[(z + step) % 4, :, 1, half[h]]

    axes = ("x", "z")
    rings = [Ring(net, axes[b], first_chunk(b), via_a.at[b], dir_a.at[b], fin_a.at[b]) for b in (0, 1)]
    core_copies = {}
    for step in (2, 1, -1, 0):
        to = (y + step) % 4
        core_copies[step] = net.copy(trans.at[to, 1 - core], core_in.at[to], net.partner())
    for r in rings:
        r.start()
    beside[0]()
    ring_y = Ring(net, "y", lambda step, h: core_in.at[(y + step) % 4, h], via_y, dir_y, fin_y)
    for step in (2, 1, -1, 0):
        core_copies[step].wait()
        to = (y + step) % 4
        core_in[to] += trans[to, core]
    ring_y.start()
    beside[1]()
    for r in rings:
        r.forward()
    beside[2]()
    ring_y.forward()
    seconds = []
    for b in (0, 1):
        for h in (0, 1):
            own = first_chunk(b)(0, h)[...]
            mid[b, :, h * 32 : h * 32 + 32, :] = own + rings[b].result(h)
        pos = z if b == 0 else x
        chunk = lambda step, h, b=b, pos=pos: mid.at[b, (pos + step) % 4, half[h]]
        r = Ring(net, axes[1 - b], chunk, via_b.at[b], dir_b.at[b], fin_b.at[b])
        r.start()
        seconds.append(r)
    beside[3]()
    for r in seconds:
        r.forward()
    beside[4]()
    for b in (0, 1):
        ring_y.result(b)
    image = []
    for b in (0, 1):
        column = core_in[y, b] + (fin_y[b] + dir_y[b])
        parts = [seconds[b].chunk(0, h)[...] + seconds[b].result(h) for h in (0, 1)]
        image.append(column + jnp.concatenate(parts, 0))
    for r in rings + seconds + [ring_y]:
        r.close()
    return jnp.concatenate(image, 1)


def split3(a):
    high = a.astype(BF16)
    rest = a - high.astype(F32)
    middle = rest.astype(BF16)
    low = (rest - middle.astype(F32)).astype(BF16)
    return jnp.concatenate([high, middle, low], 0)


class Gram:
    def __init__(self, net, fwd, rowb, direc, self_term, own, slots):
        self.net, self.fwd, self.rowb = net, fwd, rowb
        self.direc, self.self_term, self.own, self.slots = direc, self_term, own, slots

    def local(self):
        def step(k, acc):
            q, b = k // 2, k % 2
            return acc + dot(self.rowb[q // 4, q % 4, b], split3(self.fwd[q // 4, q % 4, b]), NT)

        thirds = lax.fori_loop(0, 32, step, jnp.zeros((M, 3 * M), F32))
        h = thirds[:, 0:M] + thirds[:, M : 2 * M] + thirds[:, 2 * M :]
        direc = self.direc[...]
        g = h + h.T + dot(direc * self.self_term[...], direc, NT, HI)
        self.own[0] = jnp.concatenate([g[0:32], g[32:64]], 1)
        self.copies = [self.net.copy(self.own.at[0], self.slots.at[0, 0], self.net.partner())]

    def stage(self, k):
        wait_all(self.copies)
        got = self.slots[k, 0] if k == 0 else self.slots[k, 0] + self.slots[k, 1] + self.slots[k, 2]
        self.own[k + 1] = self.own[k] + got
        if k < 3:
            self.copies = exchange(self.net, "yxz"[k], self.own.at[k + 1], self.slots.at[k + 1])

    def total(self):
        g = self.own[4]
        return jnp.concatenate([g[:, 0:M], g[:, M:]], 0)


def first_kernel(rhs, factor, weight, direc, rho, rowb, colb, part, total, *rest):
    *bufs, send, recv = rest
    net = Net(send, recv)
    net.barrier()
    resid = rhs[...]
    project(resid, factor, part)
    all_reduce_wide(net, part, total, *bufs)
    precond, rho_value = precondition(resid, factor, weight, total)
    direc[...] = precond
    rho[...] = rho_value
    gather(net, precond, rowb, colb)


def step_kernel(last, *refs):
    if last:
        (fwd, trans, row_in, direc, resid, sol, self_term, rho, sol_out, resid_out, own, slots, *rest) = refs
        bufs, (alpha_ref, send, recv) = rest[:11], rest[11:]
    else:
        (fwd, trans, row_in, direc, resid, self_term, rho, factor, weight) = refs[:9]
        (sol_out, resid_out, direc_out, rho_out, rowb, colb, own, slots, *rest) = refs[9:]
        bufs, (alpha_ref, beta_ref, part, total, *wide, send, recv) = rest[:11], rest[11:]
    net = Net(send, recv)
    gram = Gram(net, fwd, row_in, direc, self_term, own, slots)
    net.barrier()

    def local():
        gram.local()

    def after_core():
        gram.stage(0)

    def invert():
        gram.stage(1)
        if not last:
            eye = lax.broadcasted_iota(jnp.int32, (M, M), 0) == lax.broadcasted_iota(jnp.int32, (M, M), 1)
            beta_ref[...] = solve(rho[...], eye.astype(F32))

    def across():
        gram.stage(2)

    def alpha():
        gram.stage(3)
        g = gram.total()
        alpha_ref[...] = solve((g + g.T) * 0.5, rho[...])

    image = self_term[...] * direc[...] + scatter_sums(net, fwd, trans, bufs, [local, after_core, invert, across, alpha])
    step = dot(alpha_ref[...], direc[...], TN, HI)
    sol_out[...] = sol[...] + step if last else step
    residual = resid[...] - dot(alpha_ref[...], image, TN, HI)
    resid_out[...] = residual
    if not last:
        project(residual, factor, part)
        all_reduce_wide(net, part, total, *wide)
        precond, rho_value = precondition(residual, factor, weight, total)
        rho_out[...] = rho_value
        beta = dot(beta_ref[...], rho_value, NN, HI)
        fresh = precond + dot(beta, direc[...], TN, HI)
        direc_out[...] = fresh
        gather(net, fresh, rowb, colb)


def operate_kernel(count, near_rows, near_cols, far_rows, far_cols, rowb, colb, left, right, tiles, fwd, trans, held, sem):
    n = count[0]
    chunks = (n + GROUP - 1) // GROUP
    depth = held.shape[0]

    def load(k):
        return pltpu.make_async_copy(
            tiles.at[pl.ds(k * GROUP, GROUP)], held.at[lax.rem(k, depth)], sem.at[lax.rem(k, depth)]
        )

    for k in range(depth - 1):

        @pl.when(k < chunks)
        def _():
            load(k).start()

    fwd[...] = jnp.zeros_like(fwd)
    trans[...] = jnp.zeros_like(trans)

    def far(k, carry):
        out = []
        for g in range(GROUP):
            p = k * GROUP + g
            r, c = far_rows[p], far_cols[p]
            half_f = dot(colb[c], right[p], NT).astype(BF16)
            half_t = dot(rowb[r], left[p], NT).astype(BF16)
            out.append((r, c, dot(half_f, left[p]), dot(half_t, right[p])))
        for r, c, f, t in out:
            fwd[r] += f
            trans[c] += t
        return carry

    lax.fori_loop(0, left.shape[0] // GROUP, far, 0)

    def near(k, carry):
        load(k).wait()

        @pl.when(k + depth - 1 < chunks)
        def _():
            load(k + depth - 1).start()

        slot = lax.rem(k, depth)
        for g0 in range(0, GROUP, 4):
            out = []
            for g in range(g0, g0 + 4):
                s = k * GROUP + g
                r, c = near_rows[s], near_cols[s]
                tile = held[slot, g]
                valid = s < n
                f = jnp.where(valid, dot(colb[c], tile, NT), 0.0)
                t = jnp.where(valid, dot(rowb[r], tile), 0.0)
                out.append((r, c, f, t))
            for r, c, f, t in out:
                fwd[r] += f
                trans[c] += t
        return carry

    lax.fori_loop(0, chunks, near, 0)


def shape(*dims, dtype=F32):
    return jax.ShapeDtypeStruct(dims, dtype)


def wide_scratch():
    v = pltpu.VMEM
    return [
        v((M, WIDE), F32),
        v((M, WIDE), F32),
        v((32, WIDE), F32),
        v((3, 8, WIDE), F32),
        v((8, WIDE), F32),
        v((3, 8, WIDE), F32),
        v((8, WIDE), F32),
        v((3, 8, WIDE), F32),
    ]


def scatter_scratch():
    v = pltpu.VMEM
    return (
        [v((5, 32, 128), F32), v((4, 3, 32, 128), F32)]
        + [v((2, 2, 4, 32, B), F32)] * 3
        + [v((2, 4, M, B), F32)]
        + [v((2, 2, 32, B), F32)] * 3
        + [v((4, 2, M, B), F32)]
        + [v((2, M, B), F32)] * 3
    )


def sems(n):
    return [pltpu.SemaphoreType.DMA((n,)), pltpu.SemaphoreType.DMA((n,))]


def params(collective):
    return pltpu.CompilerParams(
        collective_id=collective, has_side_effects=True, vmem_limit_bytes=60 * 1024 * 1024
    )


def local(
    rhs, self_term, near_tiles, near_rows, near_cols, near_counts, far_left, far_right, far_rows, far_cols, nys_factor, nys_weight
):
    n_col = lax.axis_size("col")
    count = lax.dynamic_slice(near_counts, (lax.axis_index("row") * n_col + lax.axis_index("col"),), (1,))
    left, right = jnp.swapaxes(far_left, 1, 2), jnp.swapaxes(far_right, 1, 2)
    weight = nys_weight.reshape(1, -1)
    self_row = self_term.reshape(1, -1)
    row_shape = shape(4, 4, 2, M, B, dtype=BF16)
    col_shape = shape(4, 2, 2, M, B, dtype=BF16)
    n_wide = 1 + 3 + 3 + 3 + 3 + 1
    n_gather = 4 + 2 + 4 + 2 + 4 + 2 * 4 * 2 + 16
    n_scatter = 6 * 5 + 4 + 10

    direc, rho, rowb, colb = pl.pallas_call(
        first_kernel,
        out_shape=(shape(M, D), shape(M, M), row_shape, col_shape),
        in_specs=[VMEM] * 3,
        out_specs=(VMEM,) * 4,
        scratch_shapes=wide_scratch() + sems(n_wide + n_gather),
        compiler_params=params(0),
        name="first",
    )(rhs, nys_factor, weight)

    def operate(rowb, colb):
        fwd, trans = pl.pallas_call(
            operate_kernel,
            out_shape=(shape(32, M, B), shape(16, M, B)),
            in_specs=[SMEM] * 5 + [VMEM] * 4 + [ANY],
            out_specs=(VMEM, VMEM),
            scratch_shapes=[pltpu.VMEM((4, GROUP, B, B), BF16), pltpu.SemaphoreType.DMA((4,))],
            compiler_params=pltpu.CompilerParams(vmem_limit_bytes=60 * 1024 * 1024),
            name="operate",
        )(count, near_rows, near_cols, far_rows, far_cols, rowb.reshape(32, M, B), colb.reshape(16, M, B), left, right, near_tiles)
        return fwd.reshape(4, 4, 2, M, B), trans.reshape(4, 2, 2, M, B)

    fwd, trans = operate(rowb, colb)
    square = pltpu.VMEM((M, M), F32)
    sol, residual, direc, rho_next, rowb, colb = pl.pallas_call(
        functools.partial(step_kernel, False),
        out_shape=(shape(M, D), shape(M, D), shape(M, D), shape(M, M), row_shape, col_shape),
        in_specs=[VMEM] * 9,
        out_specs=(VMEM,) * 6,
        scratch_shapes=scatter_scratch() + [square, square] + wide_scratch() + sems(n_wide + n_gather + n_scatter),
        compiler_params=params(1),
        name="middle",
    )(fwd, trans, rowb, direc, rhs, self_row, rho, nys_factor, weight)
    fwd, trans = operate(rowb, colb)
    return pl.pallas_call(
        functools.partial(step_kernel, True),
        out_shape=(shape(M, D), shape(M, D)),
        in_specs=[VMEM] * 8,
        out_specs=(VMEM,) * 2,
        scratch_shapes=scatter_scratch() + [square] + sems(n_scatter),
        compiler_params=params(2),
        name="last",
    )(fwd, trans, rowb, direc, residual, sol, self_row, rho_next)


def solution(mesh):
    split = ("row", "col")
    in_specs = (
        P(None, split),
        P(split),
        P(split, None, None),
        P(split),
        P(split),
        P(),
        P(split, None, None),
        P(split, None, None),
        P(split),
        P(split),
        P(None, split),
        P(),
    )
    out_specs = (P(None, split), P(None, split))
    return jax.shard_map(local, mesh=mesh, in_specs=in_specs, out_specs=out_specs, check_vma=False)
```

time: 1220 us -> 193 us (0.16)
  waiting for transfers between devices: 745 us -> 0 us
  blocking collectives: 220 us -> 0 us
  Pallas kernels: 0 us -> 189 us
  other arithmetic: 108 us -> 0 us
  matrix products: 70.1 us -> 0 us
  local copies, waits for them, and re-layouts: 50.7 us -> 4.38 us
  between operations: 15.4 us -> 0.68 us
    reduce_scatter x4 -> x0, waiting for transfers between devices: 433 us -> none  [the longest x2 329 us: local(): lax.psum_scatter(row_terms, 'col', scatter_dimension=1, tiled=True)]
    psum x2 -> x0, waiting for transfers between devices: 274 us -> none  [precondition(): proj = lax.psum(local_proj, ('row', 'col'))]
    psum x3 -> x0, blocking collectives: 194 us -> none  [the longest x2 129 us: precondition(): lax.psum(jnp.dot(resid, precond.T, precision=highest), ('row', 'col'))]
    pallas_call x0 -> x5, Pallas kernels: none -> 189 us  [the longest x1 76 us: local(): pl.pallas_call(functools.partial(step_kernel, False), out_shape=(shape(M,...]
    dot_general x33 -> x0, matrix products: 68.8 us -> none  [the longest x8 19.8 us: forward_step(): jnp.einsum('gmk,gnk->gmn', col_blocks[cols], tiles, preferred_element_typ...]
    scatter-add x20 -> x0, other arithmetic: 59.9 us -> none  [the longest x2 17.8 us: local(): forward.at[far_rows]]
    all_gather x2 -> x0, waiting for transfers between devices: 38.3 us -> none  [local(): row_side = lax.all_gather(packed, 'col', axis=1, tiled=True)]
    gather x20 -> x0, local copies, waits for them, and re-layouts: 37 us -> none  [the longest x8 14.3 us: transposed_step(): row_blocks[rows]]
  transfers between devices with their start and end apart: 8 -> 0, of which waited for: 8 -> 0; matrix products, arithmetic and copies ran while one was open for 9% -> 0% of each run, Pallas kernels for 0% -> 0%
where the time goes in v1:
time: 193 us; the launch traced here: 194 us
  Pallas kernels  189 us (98%)
  local copies, waits for them, and re-layouts  4.38 us (2%)
    pallas_call x1, Pallas kernels, local(): pl.pallas_call(functools.partial(step_kernel, False), out_shape=(shape(M,...  76 us
    pallas_call x1, Pallas kernels, local(): pl.pallas_call(first_kernel, out_shape=(shape(M, D), shape(M, M), row_sha...  42.6 us
    pallas_call x1, Pallas kernels, local(): pl.pallas_call(functools.partial(step_kernel, True), out_shape=(shape(M,...  36.7 us
    pallas_call x2, Pallas kernels, operate(): pl.pallas_call(operate_kernel, out_shape=(shape(32, M, B), shape(16, M, B...  33.5 us

profile of v1, /device:TPU:0, one launch (start us, length us, event | category | flops | bytes accessed | tf_op | source)
XLA Modules:
  0.0 193.8 jit_solution(9536968258208305587)
XLA Ops:
  0.6 1.2 dynamic_slice.3.count
  1.9 42.6 %first.1 = (f32[64,512]{1,0:T(8,128)}, f32[64,64]{1,0:T(8,128)}, bf16[4,4,2,64,256]{4,3,2,1,0:T(8,128)(2,1)}, bf16[4,2,2,64,256]{4,3,2,1,0:T(8,128)(2,1)}) custom-call(f32[64,512]{1,0:T(8,128)} %refs_4_.1, f32[512,512]{1,0:T(8,128)} %refs_7_.1, f32[1,512]{1,0:T(1,128)} %bitcast.24), custom_call_target="tpu_custom_call" | custom-call | tf_op jit(solution)/shard_map/first/pallas_call | solution.py:511
  44.5 16.7 %operate.2 = (f32[32,64,256]{2,1,0:T(8,128)}, f32[16,64,256]{2,1,0:T(8,128)}) custom-call(s32[1]{0:T(128)} %dynamic_slice.3.count, s32[128]{0:T(128)} %near_rows.3, s32[128]{0:T(128)} %near_cols.3, s32[64]{0:T(128)} %far_rows.3, s32[64]{0:T(128)} %far_cols.3, bf16[32,64,256]{2,1,0:T(8,128)(2,1)} %bitcast.17, bf16[16,64,256]{2,1,0:T(8,128)(2,1)} %bitcast.23, ...), custom_call_target="tpu_custom_call" | custom-call | tf_op jit(solution)/shard_map/operate/pallas_call | solution.py:522
  61.2 76.0 %middle.1 = (f32[64,512]{1,0:T(8,128)}, f32[64,512]{1,0:T(8,128)}, f32[64,512]{1,0:T(8,128)}, f32[64,64]{1,0:T(8,128)}, bf16[4,4,2,64,256]{4,3,2,1,0:T(8,128)(2,1)}, /*index=5*/bf16[4,2,2,64,256]{4,3,2,1,0:T(8,128)(2,1)}) custom-call(f32[4,4,2,64,256]{4,3,2,1,0:T(8,128)} %bitcast.18, f32[4,2,2,64,256]{4,3,2,1,0:T(8,128)} %bitcast.20, ...), custom_call_target="tpu_custom_call" | custom-call | tf_op jit(solution)/shard_map/middle/pallas_call | solution.py:535
  137.2 16.8 %operate.3 = (f32[32,64,256]{2,1,0:T(8,128)}, f32[16,64,256]{2,1,0:T(8,128)}) custom-call(s32[1]{0:T(128)} %dynamic_slice.3.count, s32[128]{0:T(128)} %near_rows.3, s32[128]{0:T(128)} %near_cols.3, s32[64]{0:T(128)} %far_rows.3, s32[64]{0:T(128)} %far_cols.3, bf16[32,64,256]{2,1,0:T(8,128)(2,1)} %bitcast.16, bf16[16,64,256]{2,1,0:T(8,128)(2,1)} %bitcast.22, ...), custom_call_target="tpu_custom_call" | custom-call | tf_op jit(solution)/shard_map/operate/pallas_call | solution.py:522
  154.0 36.7 %last.1 = (f32[64,512]{1,0:T(8,128)}, f32[64,512]{1,0:T(8,128)}) custom-call(f32[4,4,2,64,256]{4,3,2,1,0:T(8,128)} %bitcast.19, f32[4,2,2,64,256]{4,3,2,1,0:T(8,128)} %bitcast.21, bf16[4,4,2,64,256]{4,3,2,1,0:T(8,128)(2,1)} %get-tuple-element.22.refs_2_, f32[64,512]{1,0:T(8,128)} %get-tuple-element.26.refs_3_, f32[64,512]{1,0:T(8,128)} %get-tuple-element.27.refs_4_, ...), custom_call_target="tpu_custom_call" | custom-call | tf_op jit(solution)/shard_map/last/pallas_call | solution.py:545
  190.6 1.6 copy.16
  192.2 1.6 copy.17

commit v2 on v1

--- a/solution.py
+++ b/solution.py
@@ -13,15 +13,16 @@
 BF16 = jnp.bfloat16
 VMEM = pl.BlockSpec(memory_space=pltpu.VMEM)
 SMEM = pl.BlockSpec(memory_space=pltpu.SMEM)
-ANY = pl.BlockSpec(memory_space=pl.ANY)
+HBM = pl.BlockSpec(memory_space=pltpu.HBM)
 NT = (((1,), (1,)), ((), ()))
 NN = (((1,), (0,)), ((), ()))
 TN = (((0,), (0,)), ((), ()))
 M = 64
 B = 256
 D = 512
-WIDE = 640
+CHUNK = 384
 GROUP = 8
+VMEM_LIMIT = 16 * 1024 * 1024
 
 
 def dot(a, b, dims=NN, precision=None):
@@ -45,9 +46,16 @@
             return (self.i, (self.z + step) % 4 * 4 + self.x)
         return (self.i, self.z * 4 + (self.x + step) % 4)
 
+    def plane(self):
+        steps = [(dz, dx) for dz in (0, 1, 3, 2) for dx in (0, 1, 3, 2)][1:]
+        return [(self.i, (self.z + dz) % 4 * 4 + (self.x + dx) % 4) for dz, dx in steps]
+
+    def column(self):
+        return [((self.i + d) % 8, self.j) for d in range(1, 8)]
+
     def barrier(self):
         sem = pltpu.get_barrier_semaphore()
-        peers = [self.partner()] + [self.at(a, s) for a in "xyz" for s in (1, 2, 3)]
+        peers = self.column() + self.plane()
         for peer in peers:
             pl.semaphore_signal(sem, inc=1, device_id=peer, device_id_type=MESH)
         pl.semaphore_wait(sem, len(peers))
@@ -80,37 +88,30 @@
         c.wait()
 
 
-def all_reduce_wide(net, part, total, core_in, y_in, x_own, x_in, z_own, z_in):
-    other, own = (1 - net.core) * 32, net.core * 32
-    net.copy(part.at[rows(other, 32)], core_in, net.partner()).wait()
-    core_in[...] += part[rows(own, 32), :]
-    copies = [
-        net.copy(core_in.at[rows((net.y + d) % 4 * 8, 8)], y_in.at[d - 1], net.at("y", d))
-        for d in (1, 2, 3)
-    ]
-    wait_all(copies)
-    x_own[...] = core_in[rows(net.y * 8, 8), :] + y_in[0] + y_in[1] + y_in[2]
-    wait_all(exchange(net, "x", x_own, x_in))
-    z_own[...] = x_own[...] + x_in[0] + x_in[1] + x_in[2]
-    wait_all(exchange(net, "z", z_own, z_in))
-    mine = rows(own + net.y * 8, 8)
-    total[mine, :] = z_own[...] + z_in[0] + z_in[1] + z_in[2]
-    copies = [net.copy(total.at[mine], total.at[mine], net.at("y", d)) for d in (1, 2, 3)]
-    wait_all(copies)
-    half = rows(own, 32)
-    net.copy(total.at[half], total.at[half], net.partner()).wait()
+def all_reduce_wide(net, part, total, plane_in, row_own, row_in):
+    me = net.j
+    wait_all([net.copy(part.at[p[1]], plane_in.at[k], p) for k, p in enumerate(net.plane())])
+    row_own[...] = part[me] + jnp.sum(plane_in[...], 0)
+    wait_all([net.copy(row_own, row_in.at[k], p) for k, p in enumerate(net.column())])
+    total[me] = row_own[...] + jnp.sum(row_in[...], 0)
+    wait_all([net.copy(total.at[me], total.at[me], p) for p in net.plane()])
 
 
 def project(resid, factor, part):
-    part[:, 0:D] = dot(resid, factor[...], NT, HI)
-    part[:, D:] = jnp.concatenate([dot(resid, resid, NT, HI), jnp.zeros((M, M), F32)], 1)
+    proj = dot(resid, factor[...], NT, HI)
+    inner = dot(resid, resid, NT, HI)
+    wide = jnp.concatenate([proj, inner, jnp.zeros((M, 2 * CHUNK - D - M), F32)], 1)
+    for q in range(16):
+        part[q] = wide[q // 2 * 8 : q // 2 * 8 + 8, q % 2 * CHUNK : q % 2 * CHUNK + CHUNK]
 
 
 def precondition(resid, factor, weight, total):
-    proj = total[:, 0:D]
+    lines = [jnp.concatenate([total[2 * q], total[2 * q + 1]], 1) for q in range(8)]
+    wide = jnp.concatenate(lines, 0)
+    proj = wide[:, 0:D]
     weighted = proj * weight[...]
     precond = resid + dot(weighted, factor[...], NN, HI)
-    rho = total[:, D : D + M] + dot(weighted, proj, NT, HI)
+    rho = wide[:, D : D + M] + dot(weighted, proj, NT, HI)
     return precond, rho
 
 
@@ -311,10 +312,13 @@
 
     def local(self):
         def step(k, acc):
-            q, b = k // 2, k % 2
-            return acc + dot(self.rowb[q // 4, q % 4, b], split3(self.fwd[q // 4, q % 4, b]), NT)
-
-        thirds = lax.fori_loop(0, 32, step, jnp.zeros((M, 3 * M), F32))
+            for t in range(8):
+                q = k * 4 + t // 2
+                at = (q // 4, q % 4, t % 2)
+                acc = acc + dot(self.rowb[at], split3(self.fwd[at]), NT)
+            return acc
+
+        thirds = lax.fori_loop(0, 4, step, jnp.zeros((M, 3 * M), F32))
         h = thirds[:, 0:M] + thirds[:, M : 2 * M] + thirds[:, 2 * M :]
         direc = self.direc[...]
         g = h + h.T + dot(direc * self.self_term[...], direc, NT, HI)
@@ -333,10 +337,17 @@
         return jnp.concatenate([g[:, 0:M], g[:, M:]], 0)
 
 
-def first_kernel(rhs, factor, weight, direc, rho, rowb, colb, part, total, *rest):
-    *bufs, send, recv = rest
+def first_kernel(*refs):
+    sources, (direc, rho, rowb, colb), kept = refs[:6], refs[6:10], refs[10:16]
+    part, total, *bufs, send, recv, local_sem = refs[16:]
+    rhs, factor, weight = kept[:3]
+    copies = [pltpu.make_async_copy(a, b, local_sem.at[k]) for k, (a, b) in enumerate(zip(sources, kept))]
+    for c in copies:
+        c.start()
     net = Net(send, recv)
     net.barrier()
+    for c in copies[:3]:
+        c.wait()
     resid = rhs[...]
     project(resid, factor, part)
     all_reduce_wide(net, part, total, *bufs)
@@ -344,6 +355,8 @@
     direc[...] = precond
     rho[...] = rho_value
     gather(net, precond, rowb, colb)
+    for c in copies[3:]:
+        c.wait()
 
 
 def step_kernel(last, *refs):
@@ -394,64 +407,54 @@
         gather(net, fresh, rowb, colb)
 
 
-def operate_kernel(count, near_rows, near_cols, far_rows, far_cols, rowb, colb, left, right, tiles, fwd, trans, held, sem):
-    n = count[0]
-    chunks = (n + GROUP - 1) // GROUP
-    depth = held.shape[0]
-
-    def load(k):
-        return pltpu.make_async_copy(
-            tiles.at[pl.ds(k * GROUP, GROUP)], held.at[lax.rem(k, depth)], sem.at[lax.rem(k, depth)]
-        )
-
-    for k in range(depth - 1):
-
-        @pl.when(k < chunks)
-        def _():
-            load(k).start()
-
+def operate_kernel(*refs):
+    sources, (rowb, colb, left, right, tiles, fwd, trans, half_f, half_t), tables, sem = refs[:5], refs[5:14], refs[14:19], refs[19]
+    copies = [pltpu.make_async_copy(a, b, sem.at[k]) for k, (a, b) in enumerate(zip(sources, tables))]
+    for c in copies:
+        c.start()
     fwd[...] = jnp.zeros_like(fwd)
     trans[...] = jnp.zeros_like(trans)
+    for c in copies:
+        c.wait()
+    counts, near_rows, near_cols, far_rows, far_cols = tables
+    n = counts[lax.axis_index("row") * lax.axis_size("col") + lax.axis_index("col")]
+
+    def far_halves(k, carry):
+        for g in range(16):
+            p = k * 16 + g
+            half_f[p] = dot(colb[far_cols[p]], right[p], NT).astype(BF16)
+            half_t[p] = dot(rowb[far_rows[p]], left[p], NT).astype(BF16)
+        return carry
 
     def far(k, carry):
         out = []
-        for g in range(GROUP):
-            p = k * GROUP + g
-            r, c = far_rows[p], far_cols[p]
-            half_f = dot(colb[c], right[p], NT).astype(BF16)
-            half_t = dot(rowb[r], left[p], NT).astype(BF16)
-            out.append((r, c, dot(half_f, left[p]), dot(half_t, right[p])))
+        for g in range(8):
+            p = k * 8 + g
+            out.append((far_rows[p], far_cols[p], dot(half_f[p], left[p]), dot(half_t[p], right[p])))
         for r, c, f, t in out:
             fwd[r] += f
             trans[c] += t
         return carry
 
-    lax.fori_loop(0, left.shape[0] // GROUP, far, 0)
+    lax.fori_loop(0, left.shape[0] // 16, far_halves, 0)
+    lax.fori_loop(0, left.shape[0] // 8, far, 0)
 
     def near(k, carry):
-        load(k).wait()
-
-        @pl.when(k + depth - 1 < chunks)
-        def _():
-            load(k + depth - 1).start()
-
-        slot = lax.rem(k, depth)
-        for g0 in range(0, GROUP, 4):
-            out = []
-            for g in range(g0, g0 + 4):
-                s = k * GROUP + g
-                r, c = near_rows[s], near_cols[s]
-                tile = held[slot, g]
-                valid = s < n
-                f = jnp.where(valid, dot(colb[c], tile, NT), 0.0)
-                t = jnp.where(valid, dot(rowb[r], tile), 0.0)
-                out.append((r, c, f, t))
-            for r, c, f, t in out:
-                fwd[r] += f
-                trans[c] += t
+        out = []
+        for g in range(GROUP):
+            s = k * GROUP + g
+            r, c = near_rows[s], near_cols[s]
+            tile = tiles[s]
+            valid = s < n
+            f = jnp.where(valid, dot(colb[c], tile, NT), 0.0)
+            t = jnp.where(valid, dot(rowb[r], tile), 0.0)
+            out.append((r, c, f, t))
+        for r, c, f, t in out:
+            fwd[r] += f
+            trans[c] += t
         return carry
 
-    lax.fori_loop(0, chunks, near, 0)
+    lax.fori_loop(0, (n + GROUP - 1) // GROUP, near, 0)
 
 
 def shape(*dims, dtype=F32):
@@ -461,14 +464,11 @@
 def wide_scratch():
     v = pltpu.VMEM
     return [
-        v((M, WIDE), F32),
-        v((M, WIDE), F32),
-        v((32, WIDE), F32),
-        v((3, 8, WIDE), F32),
-        v((8, WIDE), F32),
-        v((3, 8, WIDE), F32),
-        v((8, WIDE), F32),
-        v((3, 8, WIDE), F32),
+        v((16, 8, CHUNK), F32),
+        v((16, 8, CHUNK), F32),
+        v((15, 8, CHUNK), F32),
+        v((8, CHUNK), F32),
+        v((7, 8, CHUNK), F32),
     ]
 
 
@@ -490,44 +490,46 @@
 
 def params(collective):
     return pltpu.CompilerParams(
-        collective_id=collective, has_side_effects=True, vmem_limit_bytes=60 * 1024 * 1024
+        collective_id=collective, has_side_effects=True, vmem_limit_bytes=VMEM_LIMIT
     )
 
 
 def local(
     rhs, self_term, near_tiles, near_rows, near_cols, near_counts, far_left, far_right, far_rows, far_cols, nys_factor, nys_weight
 ):
-    n_col = lax.axis_size("col")
-    count = lax.dynamic_slice(near_counts, (lax.axis_index("row") * n_col + lax.axis_index("col"),), (1,))
     left, right = jnp.swapaxes(far_left, 1, 2), jnp.swapaxes(far_right, 1, 2)
     weight = nys_weight.reshape(1, -1)
     self_row = self_term.reshape(1, -1)
     row_shape = shape(4, 4, 2, M, B, dtype=BF16)
     col_shape = shape(4, 2, 2, M, B, dtype=BF16)
-    n_wide = 1 + 3 + 3 + 3 + 3 + 1
+    n_wide = 15 + 7 + 15
     n_gather = 4 + 2 + 4 + 2 + 4 + 2 * 4 * 2 + 16
     n_scatter = 6 * 5 + 4 + 10
 
-    direc, rho, rowb, colb = pl.pallas_call(
+    sources = (rhs, nys_factor, weight, near_tiles, left, right)
+    direc, rho, rowb, colb, resid, factor, weight, tiles, left, right = pl.pallas_call(
         first_kernel,
-        out_shape=(shape(M, D), shape(M, M), row_shape, col_shape),
-        in_specs=[VMEM] * 3,
-        out_specs=(VMEM,) * 4,
-        scratch_shapes=wide_scratch() + sems(n_wide + n_gather),
+        out_shape=(shape(M, D), shape(M, M), row_shape, col_shape) + tuple(shape(*a.shape, dtype=a.dtype) for a in sources),
+        in_specs=[HBM] * 6,
+        out_specs=(VMEM,) * 10,
+        scratch_shapes=wide_scratch() + sems(n_wide + n_gather) + [pltpu.SemaphoreType.DMA((6,))],
         compiler_params=params(0),
         name="first",
-    )(rhs, nys_factor, weight)
+    )(*[pltpu.with_memory_space_constraint(a, pltpu.HBM) for a in sources])
+    tables = (near_counts, near_rows, near_cols, far_rows, far_cols)
 
     def operate(rowb, colb):
         fwd, trans = pl.pallas_call(
             operate_kernel,
             out_shape=(shape(32, M, B), shape(16, M, B)),
-            in_specs=[SMEM] * 5 + [VMEM] * 4 + [ANY],
+            in_specs=[HBM] * 5 + [VMEM] * 5,
             out_specs=(VMEM, VMEM),
-            scratch_shapes=[pltpu.VMEM((4, GROUP, B, B), BF16), pltpu.SemaphoreType.DMA((4,))],
-            compiler_params=pltpu.CompilerParams(vmem_limit_bytes=60 * 1024 * 1024),
+            scratch_shapes=[pltpu.VMEM((far_left.shape[0], M, far_left.shape[2]), BF16)] * 2
+            + [pltpu.SMEM(t.shape, jnp.int32) for t in tables]
+            + [pltpu.SemaphoreType.DMA((5,))],
+            compiler_params=pltpu.CompilerParams(vmem_limit_bytes=VMEM_LIMIT),
             name="operate",
-        )(count, near_rows, near_cols, far_rows, far_cols, rowb.reshape(32, M, B), colb.reshape(16, M, B), left, right, near_tiles)
+        )(*tables, rowb.reshape(32, M, B), colb.reshape(16, M, B), left, right, tiles)
         return fwd.reshape(4, 4, 2, M, B), trans.reshape(4, 2, 2, M, B)
 
     fwd, trans = operate(rowb, colb)
@@ -540,7 +542,7 @@
         scratch_shapes=scatter_scratch() + [square, square] + wide_scratch() + sems(n_wide + n_gather + n_scatter),
         compiler_params=params(1),
         name="middle",
-    )(fwd, trans, rowb, direc, rhs, self_row, rho, nys_factor, weight)
+    )(fwd, trans, rowb, direc, resid, self_row, rho, factor, weight)
     fwd, trans = operate(rowb, colb)
     return pl.pallas_call(
         functools.partial(step_kernel, True),

time: 193 us -> 156 us (0.81)
  Pallas kernels: 189 us -> 154 us
  local copies, waits for them, and re-layouts: 4.38 us -> 1.34 us
    pallas_call x2, Pallas kernels: 33.5 us -> 10.6 us  [operate(): pl.pallas_call(operate_kernel, out_shape=(shape(32, M, B), shape(16, M, B...]
    pallas_call x1, Pallas kernels: 76 us -> 70.3 us  [local(): pl.pallas_call(functools.partial(step_kernel, False), out_shape=(shape(M,...]
    pallas_call x1, Pallas kernels: 36.7 us -> 32.5 us  [local(): pl.pallas_call(functools.partial(step_kernel, True), out_shape=(shape(M,...]
    pallas_call x1, Pallas kernels: 42.6 us -> 40.4 us  [local(): pl.pallas_call(first_kernel, out_shape=(shape(M, D), shape(M, M), row_sha...]
where the time goes in v2:
time: 156 us
  Pallas kernels  154 us (99%)
    pallas_call x1, Pallas kernels, local(): pl.pallas_call(functools.partial(step_kernel, False), out_shape=(shape(M,...  70.3 us
    pallas_call x1, Pallas kernels, local(): pl.pallas_call(first_kernel, out_shape=(shape(M, D), shape(M, M), row_sha...  40.4 us
    pallas_call x1, Pallas kernels, local(): pl.pallas_call(functools.partial(step_kernel, True), out_shape=(shape(M,...  32.5 us
    pallas_call x2, Pallas kernels, operate(): pl.pallas_call(operate_kernel, out_shape=(shape(32, M, B), shape(16, M, B...  10.6 us

profile of v2, /device:TPU:0, one launch (start us, length us, event | category | flops | bytes accessed | tf_op | source)
XLA Modules:
  0.0 155.9 jit_solution(9162403430443897496)
XLA Ops:
  0.6 0.0 copy-start.5
  0.6 0.0 copy-start.4
  0.7 0.0 copy-start.1
  0.7 0.0 copy-start.3
  0.7 0.0 copy-start.2
  0.7 0.0 copy-start
  0.7 40.4 %first.1 = (f32[64,512]{1,0:T(8,128)S(1)}, f32[64,64]{1,0:T(8,128)S(1)}, bf16[4,4,2,64,256]{4,3,2,1,0:T(8,128)(2,1)S(1)}, bf16[4,2,2,64,256]{4,3,2,1,0:T(8,128)(...) custom-call(f32[64,512]{1,0:T(8,128)} %refs_0_.3, ...), custom_call_target="tpu_custom_call" | custom-call | tf_op jit(solution)/shard_map/first/pallas_call | solution.py:510
  41.1 0.0 copy-done.5
  41.1 0.0 copy-done.4
  41.1 0.0 copy-done.1
  41.1 0.0 copy-done.3
  41.1 0.0 copy-done.2
  41.1 5.3 %operate.2 = (f32[32,64,256]{2,1,0:T(8,128)S(1)}, f32[16,64,256]{2,1,0:T(8,128)S(1)}) custom-call(s32[128]{0:T(128)S(1)} %copy-done.1, s32[128]{0:T(128)S(1)} %copy-done.2, s32[128]{0:T(128)S(1)} %copy-done.3, s32[64]{0:T(128)S(1)} %copy-done.4, s32[64]{0:T(128)S(1)} %copy-done.5, bf16[32,64,256]{2,1,0:T(8,128)(2,1)S(1)} %bitcast.13, ...), custom_call_target="tpu_custom_call" | custom-call | tf_op jit(solution)/shard_map/operate/pallas_call | solution.py:522
  46.4 0.0 copy-done
  46.5 70.3 %middle.1 = (f32[64,512]{1,0:T(8,128)S(1)}, f32[64,512]{1,0:T(8,128)S(1)}, f32[64,512]{1,0:T(8,128)S(1)}, f32[64,64]{1,0:T(8,128)S(1)}, bf16[4,4,2,64,256]{4,3,2...) custom-call(f32[4,4,2,64,256]{4,3,2,1,0:T(8,128)S(1)} %bitcast.14, f32[4,2,2,64,256]{4,3,2,1,0:T(8,128)S(1)} %bitcast.16, ...), custom_call_target="tpu_custom_call" | custom-call | tf_op jit(solution)/shard_map/middle/pallas_call | solution.py:537
  116.8 5.3 %operate.3 = (f32[32,64,256]{2,1,0:T(8,128)S(1)}, f32[16,64,256]{2,1,0:T(8,128)S(1)}) custom-call(s32[128]{0:T(128)S(1)} %copy-done.1, s32[128]{0:T(128)S(1)} %copy-done.2, s32[128]{0:T(128)S(1)} %copy-done.3, s32[64]{0:T(128)S(1)} %copy-done.4, s32[64]{0:T(128)S(1)} %copy-done.5, bf16[32,64,256]{2,1,0:T(8,128)(2,1)S(1)} %bitcast.12, ...), custom_call_target="tpu_custom_call" | custom-call | tf_op jit(solution)/shard_map/operate/pallas_call | solution.py:522
  122.1 32.5 %last.1 = (f32[64,512]{1,0:T(8,128)S(1)}, f32[64,512]{1,0:T(8,128)S(1)}) custom-call(f32[4,4,2,64,256]{4,3,2,1,0:T(8,128)S(1)} %bitcast.15, f32[4,2,2,64,256]{4,3,2,1,0:T(8,128)S(1)} %bitcast.17, bf16[4,4,2,64,256]{4,3,2,1,0:T(8,128)(2,1)S(1)} %get-tuple-element.34.refs_2_, f32[64,512]{1,0:T(8,128)S(1)} %get-tuple-element.38.refs_3_, ...), custom_call_target="tpu_custom_call" | custom-call | tf_op jit(solution)/shard_map/last/pallas_call | solution.py:547
  154.6 0.7 copy.16
  155.2 0.7 copy.17
Async XLA Ops:
  0.6 40.5 %copy-start.5 = (s32[64]{0:T(128)S(1)}, s32[64]{0:T(128)}, u32[]{:S(2)}) copy-start(s32[64]{0:T(128)} %refs_4_.3) | copy-start | bytes 772
  0.6 40.5 %copy-start.4 = (s32[64]{0:T(128)S(1)}, s32[64]{0:T(128)}, u32[]{:S(2)}) copy-start(s32[64]{0:T(128)} %refs_3_.5) | copy-start | bytes 772
  0.7 40.5 %copy-start.1 = (s32[128]{0:T(128)S(1)}, s32[128]{0:T(128)}, u32[]{:S(2)}) copy-start(s32[128]{0:T(128)} %refs_0_.5) | copy-start | bytes 1540
  0.7 40.5 %copy-start.3 = (s32[128]{0:T(128)S(1)}, s32[128]{0:T(128)}, u32[]{:S(2)}) copy-start(s32[128]{0:T(128)} %refs_2_.3) | copy-start | bytes 1540
  0.7 40.5 %copy-start.2 = (s32[128]{0:T(128)S(1)}, s32[128]{0:T(128)}, u32[]{:S(2)}) copy-start(s32[128]{0:T(128)} %refs_1_.5) | copy-start | bytes 1540
  0.7 45.8 %copy-start = (f32[512]{0:T(512)S(1)}, f32[512]{0:T(512)}, u32[]{:S(2)}) copy-start(f32[512]{0:T(512)} %param.13) | copy-start | bytes 6148

commit v3 on v2

--- a/solution.py
+++ b/solution.py
@@ -1,5 +1,3 @@
-import functools
-
 import jax
 import jax.numpy as jnp
 from jax import lax
@@ -21,7 +19,7 @@
 B = 256
 D = 512
 CHUNK = 384
-GROUP = 8
+GROUP = 16
 VMEM_LIMIT = 16 * 1024 * 1024
 
 
@@ -47,18 +45,21 @@
         return (self.i, self.z * 4 + (self.x + step) % 4)
 
     def plane(self):
-        steps = [(dz, dx) for dz in (0, 1, 3, 2) for dx in (0, 1, 3, 2)][1:]
+        steps = [(dz, dx) for dz in (2, 1, 3, 0) for dx in (2, 1, 3, 0)][:-1]
+        steps.sort(key=lambda s: -sum(min(d, 4 - d) for d in s))
         return [(self.i, (self.z + dz) % 4 * 4 + (self.x + dx) % 4) for dz, dx in steps]
 
     def column(self):
-        return [((self.i + d) % 8, self.j) for d in range(1, 8)]
-
-    def barrier(self):
-        sem = pltpu.get_barrier_semaphore()
-        peers = self.column() + self.plane()
+        others = [((self.y + d) % 4 * 2 + (self.core + c) % 2, self.j) for d in (2, 1, 3) for c in (0, 1)]
+        return others + [self.partner()]
+
+    def greet(self):
+        peers = self.plane() + self.column()
         for peer in peers:
-            pl.semaphore_signal(sem, inc=1, device_id=peer, device_id_type=MESH)
-        pl.semaphore_wait(sem, len(peers))
+            pl.semaphore_signal(pltpu.get_barrier_semaphore(), inc=1, device_id=peer, device_id_type=MESH)
+
+    def meet(self):
+        pl.semaphore_wait(pltpu.get_barrier_semaphore(), 15 + 7)
 
     def copy(self, src, dst, device):
         k = self.used
@@ -80,7 +81,7 @@
 
 
 def exchange(net, axis, src, slots):
-    return [net.copy(src, slots.at[d - 1], net.at(axis, d)) for d in (1, 2, 3)]
+    return [net.copy(src, slots.at[d - 1], net.at(axis, d)) for d in (2, 1, 3)]
 
 
 def wait_all(copies):
@@ -88,31 +89,40 @@
         c.wait()
 
 
-def all_reduce_wide(net, part, total, plane_in, row_own, row_in):
+def all_reduce_wide(net, part, total, plane_in, row_own, row_in, beside=()):
     me = net.j
-    wait_all([net.copy(part.at[p[1]], plane_in.at[k], p) for k, p in enumerate(net.plane())])
+    copies = [net.copy(part.at[p[1]], plane_in.at[k], p) for k, p in enumerate(net.plane())]
+    for step in beside[:1]:
+        step()
+    wait_all(copies)
     row_own[...] = part[me] + jnp.sum(plane_in[...], 0)
-    wait_all([net.copy(row_own, row_in.at[k], p) for k, p in enumerate(net.column())])
+    copies = [net.copy(row_own, row_in.at[k], p) for k, p in enumerate(net.column())]
+    for step in beside[1:2]:
+        step()
+    wait_all(copies)
     total[me] = row_own[...] + jnp.sum(row_in[...], 0)
-    wait_all([net.copy(total.at[me], total.at[me], p) for p in net.plane()])
-
-
-def project(resid, factor, part):
-    proj = dot(resid, factor[...], NT, HI)
-    inner = dot(resid, resid, NT, HI)
-    wide = jnp.concatenate([proj, inner, jnp.zeros((M, 2 * CHUNK - D - M), F32)], 1)
+    copies = [net.copy(total.at[me], total.at[me], p) for p in net.plane()]
+    for step in beside[2:]:
+        step()
+    wait_all(copies)
+
+
+def project(a, factor, part, others):
+    pieces = [dot(a, factor[...], NT, HI)] + [dot(a, o, NT, HI) for o in others]
+    used = D + M * len(others)
+    wide = jnp.concatenate(pieces + [jnp.zeros((M, 2 * CHUNK - used), F32)], 1)
     for q in range(16):
         part[q] = wide[q // 2 * 8 : q // 2 * 8 + 8, q % 2 * CHUNK : q % 2 * CHUNK + CHUNK]
 
 
-def precondition(resid, factor, weight, total):
-    lines = [jnp.concatenate([total[2 * q], total[2 * q + 1]], 1) for q in range(8)]
-    wide = jnp.concatenate(lines, 0)
-    proj = wide[:, 0:D]
+def assemble(total):
+    return jnp.concatenate([jnp.concatenate([total[2 * q], total[2 * q + 1]], 1) for q in range(8)], 0)
+
+
+def precondition(resid, proj, inner, factor, weight):
     weighted = proj * weight[...]
     precond = resid + dot(weighted, factor[...], NN, HI)
-    rho = wide[:, D : D + M] + dot(weighted, proj, NT, HI)
-    return precond, rho
+    return precond, inner + dot(weighted, proj, NT, HI)
 
 
 def gather(net, direc, rowb, colb):
@@ -137,12 +147,12 @@
     one = {}
     for b in (0, 1):
         ref = rowb.at[blk(b, 0, 0)]
-        one[b] = [send(ref, net.at(firsts[b], 1)), send(ref, net.at(firsts[b], -1))]
+        one[b] = [send(ref, net.at(firsts[b], step)) for step in (2, 1, -1)]
     ref = colb.at[y, core]
     col_one = [send(ref, net.at("y", 1)), send(ref, net.at("y", -1))]
     col_core = [send(ref, net.partner())]
 
-    two, second = {}, {0: {}, 1: {}}
+    second = {0: {}, 1: {}}
 
     def spread(b, first):
         ref = rowb.at[blk(b, first, 0)]
@@ -151,19 +161,15 @@
     for b in (0, 1):
         spread(b, 0)
     for b in (0, 1):
-        one[b][0].wait_recv()
-        before = rowb.at[blk(b, -1, 0)]
-        two[b] = [send(before.at[lo], net.at(firsts[b], 1))]
         one[b][1].wait_recv()
-        after = rowb.at[blk(b, 1, 0)]
-        two[b].append(send(after.at[hi], net.at(firsts[b], -1)))
+        spread(b, -1)
+    for b in (0, 1):
+        one[b][2].wait_recv()
+        spread(b, 1)
     col_one[0].wait_recv()
     col_two = [send(colb.at[(y + 3) % 4, core, 0], net.at("y", 1))]
     col_one[1].wait_recv()
     col_two.append(send(colb.at[(y + 1) % 4, core, 1], net.at("y", -1)))
-    for b in (0, 1):
-        spread(b, -1)
-        spread(b, 1)
     for step in (-1, 1):
         col_core.append(send(colb.at[(y + step) % 4, core], net.partner()))
     last = []
@@ -178,11 +184,10 @@
         last.append(send(ref.at[hi], net.at(seconds[b], -1)))
 
     for b in (0, 1):
+        one[b][0].wait_recv()
+        spread(b, 2)
+    for b in (0, 1):
         relay(b, 0)
-    for b in (0, 1):
-        two[b][0].wait_recv()
-        two[b][1].wait_recv()
-        spread(b, 2)
     for c in col_two:
         c.wait_recv()
     col_core.append(send(colb.at[(y + 2) % 4, core], net.partner()))
@@ -206,13 +211,20 @@
         self.done.append(c)
         return c
 
-    def start(self):
+    def far(self):
         chunk = self.chunk
         self.one = [self.send(chunk(2, 0), self.via.at[0], 1), self.send(chunk(2, 1), self.via.at[1], -1)]
+
+    def near(self):
+        chunk = self.chunk
         self.straight = [
             self.send(chunk(1, 1), self.direct.at[1], 1),
             self.send(chunk(-1, 0), self.direct.at[0], -1),
         ]
+
+    def start(self):
+        self.far()
+        self.near()
 
     def forward(self):
         self.two = []
@@ -231,13 +243,12 @@
             c.wait_send()
 
 
-def solve(left, right, eye=None):
+def solve(left, right):
     table = jnp.concatenate([left, right], 1)
     row_ids = lax.broadcasted_iota(jnp.int32, (M, 2 * M), 0)
     for k in range(M):
         pivot = table[k : k + 1, :] * (1.0 / table[k : k + 1, k : k + 1])
-        column = jnp.where(row_ids[:, 0:1] == k, 0.0, table[:, k : k + 1])
-        table = jnp.where(row_ids == k, pivot, table - column * pivot)
+        table = jnp.where(row_ids == k, pivot, table - table[:, k : k + 1] * pivot)
     return table[:, M:]
 
 
@@ -245,54 +256,79 @@
     via_a, dir_a, fin_a, mid, via_b, dir_b, fin_b, core_in, via_y, dir_y, fin_y = bufs
     y, z, x, core = net.y, net.z, net.x, net.core
     half = (pl.ds(0, 32), pl.ds(32, 32))
-
-    def first_chunk(b):
+    axes, order, both = ("x", "z"), (2, 1, -1, 0), (0, 1)
+    pos = (z, x)
+
+    def sub(b, s):
         if b == 0:
-            return lambda step, h: fwd.at[:, (x + step) % 4, 0, half[h]]
-        return lambda step, h: fwd.at[(z + step) % 4, :, 1, half[h]]
-
-    axes = ("x", "z")
-    rings = [Ring(net, axes[b], first_chunk(b), via_a.at[b], dir_a.at[b], fin_a.at[b]) for b in (0, 1)]
+            return lambda step, h: fwd.at[(z + s) % 4, (x + step) % 4, 0, half[h]]
+        return lambda step, h: fwd.at[(z + step) % 4, (x + s) % 4, 1, half[h]]
+
+    rings = {
+        (b, s): Ring(net, axes[b], sub(b, s), via_a.at[b, k], dir_a.at[b, k], fin_a.at[b, k])
+        for k, s in enumerate(order)
+        for b in both
+    }
+    seconds = [
+        Ring(net, axes[1 - b], lambda step, h, b=b: mid.at[b, (pos[b] + step) % 4, half[h]], via_b.at[b], dir_b.at[b], fin_b.at[b])
+        for b in both
+    ]
+    ring_y = Ring(net, "y", lambda step, h: core_in.at[(y + step) % 4, h], via_y, dir_y, fin_y)
     core_copies = {}
-    for step in (2, 1, -1, 0):
+    for step in order:
         to = (y + step) % 4
         core_copies[step] = net.copy(trans.at[to, 1 - core], core_in.at[to], net.partner())
-    for r in rings:
-        r.start()
+
+    def begin(s):
+        for b in both:
+            rings[b, s].start()
+
+    def forward(s):
+        for b in both:
+            rings[b, s].forward()
+
+    def middle(s):
+        for b in both:
+            at = (pos[b] + s) % 4
+            for h in both:
+                mid[b, at, h * 32 : h * 32 + 32, :] = sub(b, s)(0, h)[...] + rings[b, s].result(h)
+
+    begin(2)
+    begin(1)
     beside[0]()
-    ring_y = Ring(net, "y", lambda step, h: core_in.at[(y + step) % 4, h], via_y, dir_y, fin_y)
-    for step in (2, 1, -1, 0):
+    for step in order:
         core_copies[step].wait()
         to = (y + step) % 4
         core_in[to] += trans[to, core]
     ring_y.start()
+    forward(2)
+    begin(-1)
+    forward(1)
+    begin(0)
     beside[1]()
-    for r in rings:
+    middle(2)
+    for r in seconds:
+        r.far()
+    forward(-1)
+    ring_y.forward()
+    middle(1)
+    forward(0)
+    middle(-1)
+    beside[2]()
+    for r in seconds:
+        r.near()
         r.forward()
-    beside[2]()
-    ring_y.forward()
-    seconds = []
-    for b in (0, 1):
-        for h in (0, 1):
-            own = first_chunk(b)(0, h)[...]
-            mid[b, :, h * 32 : h * 32 + 32, :] = own + rings[b].result(h)
-        pos = z if b == 0 else x
-        chunk = lambda step, h, b=b, pos=pos: mid.at[b, (pos + step) % 4, half[h]]
-        r = Ring(net, axes[1 - b], chunk, via_b.at[b], dir_b.at[b], fin_b.at[b])
-        r.start()
-        seconds.append(r)
-    beside[3]()
-    for r in seconds:
-        r.forward()
-    beside[4]()
-    for b in (0, 1):
+    for b in both:
         ring_y.result(b)
+    middle(0)
+    for step in beside[3:]:
+        step()
     image = []
-    for b in (0, 1):
+    for b in both:
         column = core_in[y, b] + (fin_y[b] + dir_y[b])
-        parts = [seconds[b].chunk(0, h)[...] + seconds[b].result(h) for h in (0, 1)]
+        parts = [seconds[b].chunk(0, h)[...] + seconds[b].result(h) for h in both]
         image.append(column + jnp.concatenate(parts, 0))
-    for r in rings + seconds + [ring_y]:
+    for r in list(rings.values()) + seconds + [ring_y]:
         r.close()
     return jnp.concatenate(image, 1)
 
@@ -323,6 +359,8 @@
         direc = self.direc[...]
         g = h + h.T + dot(direc * self.self_term[...], direc, NT, HI)
         self.own[0] = jnp.concatenate([g[0:32], g[32:64]], 1)
+
+    def start(self):
         self.copies = [self.net.copy(self.own.at[0], self.slots.at[0, 0], self.net.partner())]
 
     def stage(self, k):
@@ -338,73 +376,92 @@
 
 
 def first_kernel(*refs):
-    sources, (direc, rho, rowb, colb), kept = refs[:6], refs[6:10], refs[10:16]
-    part, total, *bufs, send, recv, local_sem = refs[16:]
+    sources, (direc, rho, proj_out, inner_out, rowb, colb), kept = refs[:6], refs[6:12], refs[12:18]
+    part, total, *bufs, send, recv, local_sem = refs[18:]
     rhs, factor, weight = kept[:3]
     copies = [pltpu.make_async_copy(a, b, local_sem.at[k]) for k, (a, b) in enumerate(zip(sources, kept))]
     for c in copies:
         c.start()
     net = Net(send, recv)
-    net.barrier()
+    net.greet()
     for c in copies[:3]:
         c.wait()
     resid = rhs[...]
-    project(resid, factor, part)
+    project(resid, factor, part, [resid])
+    net.meet()
     all_reduce_wide(net, part, total, *bufs)
-    precond, rho_value = precondition(resid, factor, weight, total)
+    wide = assemble(total)
+    proj, inner = wide[:, 0:D], wide[:, D : D + M]
+    precond, rho_value = precondition(resid, proj, inner, factor, weight)
     direc[...] = precond
+    gather(net, precond, rowb, colb)
     rho[...] = rho_value
-    gather(net, precond, rowb, colb)
+    proj_out[...] = proj
+    inner_out[...] = inner
     for c in copies[3:]:
         c.wait()
 
 
-def step_kernel(last, *refs):
-    if last:
-        (fwd, trans, row_in, direc, resid, sol, self_term, rho, sol_out, resid_out, own, slots, *rest) = refs
-        bufs, (alpha_ref, send, recv) = rest[:11], rest[11:]
-    else:
-        (fwd, trans, row_in, direc, resid, self_term, rho, factor, weight) = refs[:9]
-        (sol_out, resid_out, direc_out, rho_out, rowb, colb, own, slots, *rest) = refs[9:]
-        bufs, (alpha_ref, beta_ref, part, total, *wide, send, recv) = rest[:11], rest[11:]
+def middle_kernel(
+    fwd, trans, row_in, direc, resid, self_term, rho, proj, inner, factor, weight,
+    sol_out, resid_out, direc_out, rho_out, rowb, colb, own, slots, *rest,
+):
+    bufs, (alpha_ref, turned_ref, part, total, *wide_bufs, send, recv) = rest[:11], rest[11:]
     net = Net(send, recv)
     gram = Gram(net, fwd, row_in, direc, self_term, own, slots)
-    net.barrier()
-
-    def local():
-        gram.local()
-
-    def after_core():
-        gram.stage(0)
-
-    def invert():
-        gram.stage(1)
-        if not last:
-            eye = lax.broadcasted_iota(jnp.int32, (M, M), 0) == lax.broadcasted_iota(jnp.int32, (M, M), 1)
-            beta_ref[...] = solve(rho[...], eye.astype(F32))
-
-    def across():
-        gram.stage(2)
+    net.greet()
+    gram.local()
+    net.meet()
+    gram.start()
+    steps = [lambda: gram.stage(0), lambda: gram.stage(1), lambda: gram.stage(2)]
+    image = self_term[...] * direc[...] + scatter_sums(net, fwd, trans, bufs, steps)
+    project(image, factor, part, [resid[...], image])
 
     def alpha():
         gram.stage(3)
         g = gram.total()
         alpha_ref[...] = solve((g + g.T) * 0.5, rho[...])
 
-    image = self_term[...] * direc[...] + scatter_sums(net, fwd, trans, bufs, [local, after_core, invert, across, alpha])
-    step = dot(alpha_ref[...], direc[...], TN, HI)
-    sol_out[...] = sol[...] + step if last else step
-    residual = resid[...] - dot(alpha_ref[...], image, TN, HI)
-    resid_out[...] = residual
-    if not last:
-        project(residual, factor, part)
-        all_reduce_wide(net, part, total, *wide)
-        precond, rho_value = precondition(residual, factor, weight, total)
-        rho_out[...] = rho_value
-        beta = dot(beta_ref[...], rho_value, NN, HI)
-        fresh = precond + dot(beta, direc[...], TN, HI)
-        direc_out[...] = fresh
-        gather(net, fresh, rowb, colb)
+    def update():
+        resid_out[...] = resid[...] - dot(alpha_ref[...], image, TN, HI)
+        sol_out[...] = dot(alpha_ref[...], direc[...], TN, HI)
+
+    def turn():
+        eye = lax.broadcasted_iota(jnp.int32, (M, M), 0) == lax.broadcasted_iota(jnp.int32, (M, M), 1)
+        turned_ref[...] = dot(solve(rho[...], eye.astype(F32)), direc[...], TN, HI)
+
+    all_reduce_wide(net, part, total, *wide_bufs, beside=(alpha, update, turn))
+    step = alpha_ref[...]
+    wide = assemble(total)
+    across = dot(step, wide[:, D : D + M], TN, HI)
+    own_part = dot(step, dot(wide[:, D + M : D + 2 * M], step, NN, HI), TN, HI)
+    new_inner = inner[...] - across - across.T + own_part
+    new_proj = proj[...] - dot(step, wide[:, 0:D], TN, HI)
+    precond, rho_value = precondition(resid_out[...], new_proj, new_inner, factor, weight)
+    fresh = precond + dot(rho_value, turned_ref[...], TN, HI)
+    direc_out[...] = fresh
+    gather(net, fresh, rowb, colb)
+    rho_out[...] = rho_value
+
+
+def last_kernel(fwd, trans, row_in, direc, resid, sol, self_term, rho, sol_out, resid_out, own, slots, *rest):
+    bufs, (alpha_ref, send, recv) = rest[:11], rest[11:]
+    net = Net(send, recv)
+    gram = Gram(net, fwd, row_in, direc, self_term, own, slots)
+    net.greet()
+    gram.local()
+    net.meet()
+    gram.start()
+
+    def alpha():
+        gram.stage(3)
+        g = gram.total()
+        alpha_ref[...] = solve((g + g.T) * 0.5, rho[...])
+        sol_out[...] = sol[...] + dot(alpha_ref[...], direc[...], TN, HI)
+
+    steps = [lambda: gram.stage(0), lambda: gram.stage(1), lambda: gram.stage(2), alpha]
+    image = self_term[...] * direc[...] + scatter_sums(net, fwd, trans, bufs, steps)
+    resid_out[...] = resid[...] - dot(alpha_ref[...], image, TN, HI)
 
 
 def operate_kernel(*refs):
@@ -428,8 +485,8 @@
 
     def far(k, carry):
         out = []
-        for g in range(8):
-            p = k * 8 + g
+        for g in range(32):
+            p = k * 32 + g
             out.append((far_rows[p], far_cols[p], dot(half_f[p], left[p]), dot(half_t[p], right[p])))
         for r, c, f, t in out:
             fwd[r] += f
@@ -437,7 +494,7 @@
         return carry
 
     lax.fori_loop(0, left.shape[0] // 16, far_halves, 0)
-    lax.fori_loop(0, left.shape[0] // 8, far, 0)
+    lax.fori_loop(0, left.shape[0] // 32, far, 0)
 
     def near(k, carry):
         out = []
@@ -476,7 +533,7 @@
     v = pltpu.VMEM
     return (
         [v((5, 32, 128), F32), v((4, 3, 32, 128), F32)]
-        + [v((2, 2, 4, 32, B), F32)] * 3
+        + [v((2, 4, 2, 32, B), F32)] * 3
         + [v((2, 4, M, B), F32)]
         + [v((2, 2, 32, B), F32)] * 3
         + [v((4, 2, M, B), F32)]
@@ -503,15 +560,15 @@
     row_shape = shape(4, 4, 2, M, B, dtype=BF16)
     col_shape = shape(4, 2, 2, M, B, dtype=BF16)
     n_wide = 15 + 7 + 15
-    n_gather = 4 + 2 + 4 + 2 + 4 + 2 * 4 * 2 + 16
-    n_scatter = 6 * 5 + 4 + 10
+    n_gather = 2 * 3 + 2 * 2 + 4 + 2 * 4 * 2 * 2
+    n_scatter = 6 * 8 + 6 * 3 + 4 + 10
 
     sources = (rhs, nys_factor, weight, near_tiles, left, right)
-    direc, rho, rowb, colb, resid, factor, weight, tiles, left, right = pl.pallas_call(
+    direc, rho, proj, inner, rowb, colb, resid, factor, weight, tiles, left, right = pl.pallas_call(
         first_kernel,
-        out_shape=(shape(M, D), shape(M, M), row_shape, col_shape) + tuple(shape(*a.shape, dtype=a.dtype) for a in sources),
+        out_shape=(shape(M, D), shape(M, M), shape(M, D), shape(M, M), row_shape, col_shape) + tuple(shape(*a.shape, dtype=a.dtype) for a in sources),
         in_specs=[HBM] * 6,
-        out_specs=(VMEM,) * 10,
+        out_specs=(VMEM,) * 12,
         scratch_shapes=wide_scratch() + sems(n_wide + n_gather) + [pltpu.SemaphoreType.DMA((6,))],
         compiler_params=params(0),
         name="first",
@@ -535,17 +592,17 @@
     fwd, trans = operate(rowb, colb)
     square = pltpu.VMEM((M, M), F32)
     sol, residual, direc, rho_next, rowb, colb = pl.pallas_call(
-        functools.partial(step_kernel, False),
+        middle_kernel,
         out_shape=(shape(M, D), shape(M, D), shape(M, D), shape(M, M), row_shape, col_shape),
-        in_specs=[VMEM] * 9,
+        in_specs=[VMEM] * 11,
         out_specs=(VMEM,) * 6,
-        scratch_shapes=scatter_scratch() + [square, square] + wide_scratch() + sems(n_wide + n_gather + n_scatter),
+        scratch_shapes=scatter_scratch() + [square, pltpu.VMEM((M, D), F32)] + wide_scratch() + sems(n_wide + n_gather + n_scatter),
         compiler_params=params(1),
         name="middle",
-    )(fwd, trans, rowb, direc, resid, self_row, rho, factor, weight)
+    )(fwd, trans, rowb, direc, resid, self_row, rho, proj, inner, factor, weight)
     fwd, trans = operate(rowb, colb)
     return pl.pallas_call(
-        functools.partial(step_kernel, True),
+        last_kernel,
         out_shape=(shape(M, D), shape(M, D)),
         in_specs=[VMEM] * 8,
         out_specs=(VMEM,) * 2,

time: 156 us -> 140 us (0.90)
  Pallas kernels: 154 us -> 138 us
    pallas_call x3, Pallas kernels: 143 us -> 115 us  [the longest x1 52.6 us: local(): pl.pallas_call(middle_kernel, out_shape=(shape(M, D), shape(M, D), shape(...]
    pallas_call x2, Pallas kernels: 10.6 us -> 23.5 us  [operate(): pl.pallas_call(operate_kernel, out_shape=(shape(32, M, B), shape(16, M, B...]
where the time goes in v3:
time: 140 us
  Pallas kernels  138 us (99%)
    pallas_call x1, Pallas kernels, local(): pl.pallas_call(middle_kernel, out_shape=(shape(M, D), shape(M, D), shape(...  52.6 us
    pallas_call x1, Pallas kernels, local(): pl.pallas_call(first_kernel, out_shape=(shape(M, D), shape(M, M), shape(M...  35.7 us
    pallas_call x1, Pallas kernels, local(): pl.pallas_call(last_kernel, out_shape=(shape(M, D), shape(M, D)), in_spec...  26.3 us
    pallas_call x2, Pallas kernels, operate(): pl.pallas_call(operate_kernel, out_shape=(shape(32, M, B), shape(16, M, B...  23.5 us

profile of v3, /device:TPU:0, one launch (start us, length us, event | category | flops | bytes accessed | tf_op | source)
XLA Modules:
  0.0 140.1 jit_solution(10587685639584161125)
XLA Ops:
  0.6 0.0 copy-start.5
  0.6 0.0 copy-start.4
  0.7 0.0 copy-start.1
  0.7 0.0 copy-start.3
  0.7 0.0 copy-start.2
  0.7 0.0 copy-start
  0.7 35.7 %first.1 = (f32[64,512]{1,0:T(8,128)S(1)}, f32[64,64]{1,0:T(8,128)S(1)}, f32[64,512]{1,0:T(8,128)S(1)}, f32[64,64]{1,0:T(8,128)S(1)}, bf16[4,4,2,64,256]{4,3,2,1...) custom-call(f32[64,512]{1,0:T(8,128)} %refs_0_.3, ...), custom_call_target="tpu_custom_call" | custom-call | tf_op jit(solution)/shard_map/first/pallas_call | solution.py:567
  36.4 0.0 copy-done.5
  36.4 0.0 copy-done.4
  36.4 0.0 copy-done.1
  36.4 0.0 copy-done.3
  36.4 0.0 copy-done.2
  36.4 11.7 %operate.2 = (f32[32,64,256]{2,1,0:T(8,128)S(1)}, f32[16,64,256]{2,1,0:T(8,128)S(1)}) custom-call(s32[128]{0:T(128)S(1)} %copy-done.1, s32[128]{0:T(128)S(1)} %copy-done.2, s32[128]{0:T(128)S(1)} %copy-done.3, s32[64]{0:T(128)S(1)} %copy-done.4, s32[64]{0:T(128)S(1)} %copy-done.5, bf16[32,64,256]{2,1,0:T(8,128)(2,1)S(1)} %bitcast.12, ...), custom_call_target="tpu_custom_call" | custom-call | tf_op jit(solution)/shard_map/operate/pallas_call | solution.py:579
  48.2 0.0 copy-done
  48.2 52.6 %middle.1 = (f32[64,512]{1,0:T(8,128)S(1)}, f32[64,512]{1,0:T(8,128)S(1)}, f32[64,512]{1,0:T(8,128)S(1)}, f32[64,64]{1,0:T(8,128)S(1)}, bf16[4,4,2,64,256]{4,3,2...) custom-call(f32[4,4,2,64,256]{4,3,2,1,0:T(8,128)S(1)} %bitcast.14, f32[4,2,2,64,256]{4,3,2,1,0:T(8,128)S(1)} %bitcast.16, ...), custom_call_target="tpu_custom_call" | custom-call | tf_op jit(solution)/shard_map/middle/pallas_call | solution.py:594
  100.8 11.8 %operate.3 = (f32[32,64,256]{2,1,0:T(8,128)S(1)}, f32[16,64,256]{2,1,0:T(8,128)S(1)}) custom-call(s32[128]{0:T(128)S(1)} %copy-done.1, s32[128]{0:T(128)S(1)} %copy-done.2, s32[128]{0:T(128)S(1)} %copy-done.3, s32[64]{0:T(128)S(1)} %copy-done.4, s32[64]{0:T(128)S(1)} %copy-done.5, bf16[32,64,256]{2,1,0:T(8,128)(2,1)S(1)} %bitcast.13, ...), custom_call_target="tpu_custom_call" | custom-call | tf_op jit(solution)/shard_map/operate/pallas_call | solution.py:579
  112.5 26.3 %last.1 = (f32[64,512]{1,0:T(8,128)S(1)}, f32[64,512]{1,0:T(8,128)S(1)}) custom-call(f32[4,4,2,64,256]{4,3,2,1,0:T(8,128)S(1)} %bitcast.15, f32[4,2,2,64,256]{4,3,2,1,0:T(8,128)S(1)} %bitcast.17, bf16[4,4,2,64,256]{4,3,2,1,0:T(8,128)(2,1)S(1)} %get-tuple-element.38.row_in, f32[64,512]{1,0:T(8,128)S(1)} %get-tuple-element.42.direc, ...), custom_call_target="tpu_custom_call" | custom-call | tf_op jit(solution)/shard_map/last/pallas_call | solution.py:604
  138.8 0.7 copy.16
  139.5 0.7 copy.17
Async XLA Ops:
  0.6 35.7 %copy-start.5 = (s32[64]{0:T(128)S(1)}, s32[64]{0:T(128)}, u32[]{:S(2)}) copy-start(s32[64]{0:T(128)} %refs_4_.3) | copy-start | bytes 772
  0.6 35.7 %copy-start.4 = (s32[64]{0:T(128)S(1)}, s32[64]{0:T(128)}, u32[]{:S(2)}) copy-start(s32[64]{0:T(128)} %refs_3_.5) | copy-start | bytes 772
  0.7 35.7 %copy-start.1 = (s32[128]{0:T(128)S(1)}, s32[128]{0:T(128)}, u32[]{:S(2)}) copy-start(s32[128]{0:T(128)} %refs_0_.5) | copy-start | bytes 1540
  0.7 35.7 %copy-start.3 = (s32[128]{0:T(128)S(1)}, s32[128]{0:T(128)}, u32[]{:S(2)}) copy-start(s32[128]{0:T(128)} %refs_2_.3) | copy-start | bytes 1540
  0.7 35.7 %copy-start.2 = (s32[128]{0:T(128)S(1)}, s32[128]{0:T(128)}, u32[]{:S(2)}) copy-start(s32[128]{0:T(128)} %refs_1_.5) | copy-start | bytes 1540
  0.7 47.5 %copy-start = (f32[512]{0:T(512)S(1)}, f32[512]{0:T(512)}, u32[]{:S(2)}) copy-start(f32[512]{0:T(512)} %param.13) | copy-start | bytes 6148

commit v4 on v3

--- a/solution.py
+++ b/solution.py
@@ -20,6 +20,7 @@
 D = 512
 CHUNK = 384
 GROUP = 16
+ROUTED = (2, 1, -1)
 VMEM_LIMIT = 16 * 1024 * 1024
 
 
@@ -49,17 +50,16 @@
         steps.sort(key=lambda s: -sum(min(d, 4 - d) for d in s))
         return [(self.i, (self.z + dz) % 4 * 4 + (self.x + dx) % 4) for dz, dx in steps]
 
-    def column(self):
-        others = [((self.y + d) % 4 * 2 + (self.core + c) % 2, self.j) for d in (2, 1, 3) for c in (0, 1)]
-        return others + [self.partner()]
-
-    def greet(self):
-        peers = self.plane() + self.column()
+    def lines(self):
+        return [self.at(a, s) for a in "xyz" for s in (2, 1, 3)] + [self.partner()]
+
+    def greet(self, peers):
+        self.greeted = len(peers)
         for peer in peers:
             pl.semaphore_signal(pltpu.get_barrier_semaphore(), inc=1, device_id=peer, device_id_type=MESH)
 
     def meet(self):
-        pl.semaphore_wait(pltpu.get_barrier_semaphore(), 15 + 7)
+        pl.semaphore_wait(pltpu.get_barrier_semaphore(), self.greeted)
 
     def copy(self, src, dst, device):
         k = self.used
@@ -89,18 +89,20 @@
         c.wait()
 
 
-def all_reduce_wide(net, part, total, plane_in, row_own, row_in, beside=()):
+def all_reduce_wide(net, part, total, plane_in, row_own, row_in, row_both, beside=()):
     me = net.j
     copies = [net.copy(part.at[p[1]], plane_in.at[k], p) for k, p in enumerate(net.plane())]
     for step in beside[:1]:
         step()
     wait_all(copies)
     row_own[...] = part[me] + jnp.sum(plane_in[...], 0)
-    copies = [net.copy(row_own, row_in.at[k], p) for k, p in enumerate(net.column())]
+    net.copy(row_own, row_in.at[3], net.partner()).wait()
+    row_both[...] = row_own[...] + row_in[3]
+    copies = exchange(net, "y", row_both, row_in)
     for step in beside[1:2]:
         step()
     wait_all(copies)
-    total[me] = row_own[...] + jnp.sum(row_in[...], 0)
+    total[me] = row_both[...] + row_in[0] + row_in[1] + row_in[2]
     copies = [net.copy(total.at[me], total.at[me], p) for p in net.plane()]
     for step in beside[2:]:
         step()
@@ -156,7 +158,8 @@
 
     def spread(b, first):
         ref = rowb.at[blk(b, first, 0)]
-        second[b][first] = [send(ref, net.at(seconds[b], 1)), send(ref, net.at(seconds[b], -1))]
+        steps = (2, 1, -1) if first in ROUTED else (1, -1)
+        second[b][first] = [send(ref, net.at(seconds[b], step)) for step in steps]
 
     for b in (0, 1):
         spread(b, 0)
@@ -175,6 +178,9 @@
     last = []
 
     def relay(b, first):
+        if first in ROUTED:
+            last.extend(second[b][first])
+            return
         up, down = second[b][first]
         up.wait_recv()
         ref = rowb.at[blk(b, first, -1)]
@@ -383,7 +389,7 @@
     for c in copies:
         c.start()
     net = Net(send, recv)
-    net.greet()
+    net.greet(net.plane() + [net.at("y", s) for s in (2, 1, 3)] + [net.partner()])
     for c in copies[:3]:
         c.wait()
     resid = rhs[...]
@@ -409,7 +415,7 @@
     bufs, (alpha_ref, turned_ref, part, total, *wide_bufs, send, recv) = rest[:11], rest[11:]
     net = Net(send, recv)
     gram = Gram(net, fwd, row_in, direc, self_term, own, slots)
-    net.greet()
+    net.greet(net.lines())
     gram.local()
     net.meet()
     gram.start()
@@ -448,7 +454,7 @@
     bufs, (alpha_ref, send, recv) = rest[:11], rest[11:]
     net = Net(send, recv)
     gram = Gram(net, fwd, row_in, direc, self_term, own, slots)
-    net.greet()
+    net.greet(net.lines())
     gram.local()
     net.meet()
     gram.start()
@@ -525,7 +531,8 @@
         v((16, 8, CHUNK), F32),
         v((15, 8, CHUNK), F32),
         v((8, CHUNK), F32),
-        v((7, 8, CHUNK), F32),
+        v((4, 8, CHUNK), F32),
+        v((8, CHUNK), F32),
     ]
 
 
@@ -559,8 +566,8 @@
     self_row = self_term.reshape(1, -1)
     row_shape = shape(4, 4, 2, M, B, dtype=BF16)
     col_shape = shape(4, 2, 2, M, B, dtype=BF16)
-    n_wide = 15 + 7 + 15
-    n_gather = 2 * 3 + 2 * 2 + 4 + 2 * 4 * 2 * 2
+    n_wide = 15 + 4 + 15
+    n_gather = 2 * 3 + 2 * 2 + 4 + 2 * (3 * 3 + 4)
     n_scatter = 6 * 8 + 6 * 3 + 4 + 10
 
     sources = (rhs, nys_factor, weight, near_tiles, left, right)

time: 140 us -> 134 us (0.957)
  Pallas kernels: 138 us -> 132 us
    pallas_call x2, Pallas kernels: 23.5 us -> 10.1 us  [operate(): pl.pallas_call(operate_kernel, out_shape=(shape(32, M, B), shape(16, M, B...]
    pallas_call x1, Pallas kernels: 26.3 us -> 32.6 us  [local(): pl.pallas_call(last_kernel, out_shape=(shape(M, D), shape(M, D)), in_spec...]
    pallas_call x1, Pallas kernels: 52.6 us -> 55.1 us  [local(): pl.pallas_call(middle_kernel, out_shape=(shape(M, D), shape(M, D), shape(...]
where the time goes in v4:
time: 134 us
  Pallas kernels  132 us (99%)
  local copies, waits for them, and re-layouts  1.34 us (1%)
    pallas_call x1, Pallas kernels, local(): pl.pallas_call(middle_kernel, out_shape=(shape(M, D), shape(M, D), shape(...  55.1 us
    pallas_call x1, Pallas kernels, local(): pl.pallas_call(first_kernel, out_shape=(shape(M, D), shape(M, M), shape(M...  34.3 us
    pallas_call x1, Pallas kernels, local(): pl.pallas_call(last_kernel, out_shape=(shape(M, D), shape(M, D)), in_spec...  32.6 us
    pallas_call x2, Pallas kernels, operate(): pl.pallas_call(operate_kernel, out_shape=(shape(32, M, B), shape(16, M, B...  10.1 us

profile of v4, /device:TPU:0, one launch (start us, length us, event | category | flops | bytes accessed | tf_op | source)
XLA Modules:
  0.0 134.1 jit_solution(11214604258081791229)
XLA Ops:
  0.6 0.0 copy-start.5
  0.6 0.0 copy-start.4
  0.7 0.0 copy-start.1
  0.7 0.0 copy-start.3
  0.7 0.0 copy-start.2
  0.7 0.0 copy-start
  0.7 34.3 %first.1 = (f32[64,512]{1,0:T(8,128)S(1)}, f32[64,64]{1,0:T(8,128)S(1)}, f32[64,512]{1,0:T(8,128)S(1)}, f32[64,64]{1,0:T(8,128)S(1)}, bf16[4,4,2,64,256]{4,3,2,1...) custom-call(f32[64,512]{1,0:T(8,128)} %refs_0_.3, ...), custom_call_target="tpu_custom_call" | custom-call | tf_op jit(solution)/shard_map/first/pallas_call | solution.py:574
  35.0 0.0 copy-done.5
  35.0 0.0 copy-done.4
  35.0 0.0 copy-done.1
  35.0 0.0 copy-done.3
  35.0 0.0 copy-done.2
  35.1 5.0 %operate.2 = (f32[32,64,256]{2,1,0:T(8,128)S(1)}, f32[16,64,256]{2,1,0:T(8,128)S(1)}) custom-call(s32[128]{0:T(128)S(1)} %copy-done.1, s32[128]{0:T(128)S(1)} %copy-done.2, s32[128]{0:T(128)S(1)} %copy-done.3, s32[64]{0:T(128)S(1)} %copy-done.4, s32[64]{0:T(128)S(1)} %copy-done.5, bf16[32,64,256]{2,1,0:T(8,128)(2,1)S(1)} %bitcast.12, ...), custom_call_target="tpu_custom_call" | custom-call | tf_op jit(solution)/shard_map/operate/pallas_call | solution.py:586
  40.1 0.0 copy-done
  40.1 55.1 %middle.1 = (f32[64,512]{1,0:T(8,128)S(1)}, f32[64,512]{1,0:T(8,128)S(1)}, f32[64,512]{1,0:T(8,128)S(1)}, f32[64,64]{1,0:T(8,128)S(1)}, bf16[4,4,2,64,256]{4,3,2...) custom-call(f32[4,4,2,64,256]{4,3,2,1,0:T(8,128)S(1)} %bitcast.14, f32[4,2,2,64,256]{4,3,2,1,0:T(8,128)S(1)} %bitcast.16, ...), custom_call_target="tpu_custom_call" | custom-call | tf_op jit(solution)/shard_map/middle/pallas_call | solution.py:601
  95.2 5.0 %operate.3 = (f32[32,64,256]{2,1,0:T(8,128)S(1)}, f32[16,64,256]{2,1,0:T(8,128)S(1)}) custom-call(s32[128]{0:T(128)S(1)} %copy-done.1, s32[128]{0:T(128)S(1)} %copy-done.2, s32[128]{0:T(128)S(1)} %copy-done.3, s32[64]{0:T(128)S(1)} %copy-done.4, s32[64]{0:T(128)S(1)} %copy-done.5, bf16[32,64,256]{2,1,0:T(8,128)(2,1)S(1)} %bitcast.13, ...), custom_call_target="tpu_custom_call" | custom-call | tf_op jit(solution)/shard_map/operate/pallas_call | solution.py:586
  100.2 32.6 %last.1 = (f32[64,512]{1,0:T(8,128)S(1)}, f32[64,512]{1,0:T(8,128)S(1)}) custom-call(f32[4,4,2,64,256]{4,3,2,1,0:T(8,128)S(1)} %bitcast.15, f32[4,2,2,64,256]{4,3,2,1,0:T(8,128)S(1)} %bitcast.17, bf16[4,4,2,64,256]{4,3,2,1,0:T(8,128)(2,1)S(1)} %get-tuple-element.38.row_in, f32[64,512]{1,0:T(8,128)S(1)} %get-tuple-element.42.direc, ...), custom_call_target="tpu_custom_call" | custom-call | tf_op jit(solution)/shard_map/last/pallas_call | solution.py:611
  132.8 0.7 copy.16
  133.4 0.7 copy.17
Async XLA Ops:
  0.6 34.4 %copy-start.5 = (s32[64]{0:T(128)S(1)}, s32[64]{0:T(128)}, u32[]{:S(2)}) copy-start(s32[64]{0:T(128)} %refs_4_.3) | copy-start | bytes 772
  0.6 34.4 %copy-start.4 = (s32[64]{0:T(128)S(1)}, s32[64]{0:T(128)}, u32[]{:S(2)}) copy-start(s32[64]{0:T(128)} %refs_3_.5) | copy-start | bytes 772
  0.7 34.4 %copy-start.1 = (s32[128]{0:T(128)S(1)}, s32[128]{0:T(128)}, u32[]{:S(2)}) copy-start(s32[128]{0:T(128)} %refs_0_.5) | copy-start | bytes 1540
  0.7 34.4 %copy-start.3 = (s32[128]{0:T(128)S(1)}, s32[128]{0:T(128)}, u32[]{:S(2)}) copy-start(s32[128]{0:T(128)} %refs_2_.3) | copy-start | bytes 1540
  0.7 34.4 %copy-start.2 = (s32[128]{0:T(128)S(1)}, s32[128]{0:T(128)}, u32[]{:S(2)}) copy-start(s32[128]{0:T(128)} %refs_1_.5) | copy-start | bytes 1540
  0.7 39.4 %copy-start = (f32[512]{0:T(512)S(1)}, f32[512]{0:T(512)}, u32[]{:S(2)}) copy-start(f32[512]{0:T(512)} %param.13) | copy-start | bytes 6148
